TPU v7x, 32 devices: a whole 2x2x4 slice. The times are simulated.
32 devices in a mesh: aux: 8 (over y, x, core), orb: 4 (over z).
Axes of the slice: x: 2, y: 2, z: 4, core: 2. Of those that a mesh axis runs over, the one named last changes fastest.
Arguments:
- tiles: float32 [256, 64, 4096], P(('aux', 'orb')), may hold values from -6 to 6
- tile_list: int32 [4, 256], P(None, ('aux', 'orb')), may hold values from 0 to 255, as said below
- orb_factor: float32 [4096, 256], P('orb'), may hold values from -30 to 30
- nu_factor: float32 [512, 256], replicated, may hold values from -30 to 30
Outputs:
- aux_factor: float32 [16384, 256], P('aux')
- orb_updated: float32 [4096, 256], P('orb')
- nu_updated: float32 [512, 256], replicated
Inputs may be any that keep to these rules, and one draw needn't show every extreme that they name: `tile_list`: slot s belongs to the device s // 8 along aux+orb; for that device with aux index a and orb index o, row 0 lies in [a * 32, (a + 1) * 32), row 1 in [o * 16, (o + 1) * 16), row 2 below 8. The coordinates of one device's slots are distinct. Row 3 is 0 or 1: 1 on a device's first slots and 0 on the rest; every device has at least one flagged slot and some device has all 8 flagged.
All inputs are finite; a program needn't handle non-finite values.
Results may differ from a plain program's by a relative error of at most 0.0003.
Values sent between devices are 32-bit elements; how exact they have to be, the bound alone decides.
A program may use at most 256 MiB of HBM per device.

v0:
```python
import functools

import jax
import jax.numpy as jnp
from jax import lax
from jax.experimental import pallas as pl
from jax.experimental.pallas import tpu as pltpu
from jax.sharding import PartitionSpec as P

P_SIZE = 16384
MU = 4096
NU = 512

ridge_weight = 0.5
epsilon = 1e-06
highest = lax.Precision.HIGHEST
f32 = jnp.float32
bf16 = jnp.bfloat16
PANEL = 32


MESH = pl.DeviceIdType.MESH


def reduce_kernel(steps, x_ref, out_ref, sum_ref, all_ref, *scratch):
    count = len(steps)
    landing = scratch[:count]
    send_sem, recv_sem = scratch[count:]
    bits, partners = [], []
    for axis, bit in steps:
        here = lax.axis_index(axis)
        value = (here // (1 << bit)) % 2
        bits.append(value)
        partners.append({axis: here + (1 - 2 * value) * (1 << bit)})
    barrier = pltpu.get_barrier_semaphore()
    for partner in partners:
        pl.semaphore_signal(barrier, inc=1, device_id=partner, device_id_type=MESH)
    pl.semaphore_wait(barrier, count)
    sum_ref[...] = x_ref[...]
    length = sum_ref.shape[0]
    start = jnp.int32(0)
    kept = []
    for step in range(count):
        length //= 2
        mine = pl.multiple_of(start + bits[step] * length, 8)
        other = pl.multiple_of(start + (1 - bits[step]) * length, 8)
        copy = pltpu.make_async_remote_copy(
            src_ref=sum_ref.at[pl.ds(other, length), :],
            dst_ref=landing[step],
            send_sem=send_sem.at[step],
            recv_sem=recv_sem.at[step],
            device_id=partners[step],
            device_id_type=MESH,
        )
        copy.start()
        copy.wait()
        sum_ref[pl.ds(mine, length), :] += landing[step][...]
        start = mine
        kept.append((mine, length))
    mine, length = kept[-1]
    all_ref[pl.ds(mine, length), :] = sum_ref[pl.ds(mine, length), :]
    for step in reversed(range(count)):
        mine, length = kept[step]
        rows = all_ref.at[pl.ds(mine, length), :]
        copy = pltpu.make_async_remote_copy(
            src_ref=rows,
            dst_ref=rows,
            send_sem=send_sem.at[count + step],
            recv_sem=recv_sem.at[count + step],
            device_id=partners[step],
            device_id_type=MESH,
        )
        copy.start()
        copy.wait()
    out_ref[...] = all_ref[...]


def all_reduce(x, axes, number, name):
    steps = []
    for axis in axes:
        size = lax.axis_size(axis)
        if size & (size - 1):
            return lax.psum(x, axes)
        steps += [(axis, bit) for bit in range(size.bit_length() - 1)]
    rows, columns = x.shape
    if rows % (8 << len(steps)):
        return lax.psum(x, axes)
    count = len(steps)
    vmem = pl.BlockSpec(memory_space=pltpu.VMEM)
    return pl.pallas_call(
        functools.partial(reduce_kernel, tuple(steps)),
        out_shape=jax.ShapeDtypeStruct(x.shape, f32),
        in_specs=[vmem],
        out_specs=vmem,
        scratch_shapes=[pltpu.VMEM((rows, columns), f32)] * 2
        + [pltpu.VMEM((rows >> (step + 1), columns), f32) for step in range(count)]
        + [pltpu.SemaphoreType.DMA((2 * count,)), pltpu.SemaphoreType.DMA((2 * count,))],
        compiler_params=pltpu.CompilerParams(collective_id=number, has_side_effects=True),
        name=name,
    )(x)


def gram_of(matrix):
    return jnp.dot(matrix.T, matrix, precision=highest, preferred_element_type=f32)


def split_two(x):
    high = x.astype(bf16)
    return high, (x - high.astype(f32)).astype(bf16)


def split_three(x):
    high = x.astype(bf16)
    rest = x - high.astype(f32)
    middle = rest.astype(bf16)
    return high, middle, (rest - middle.astype(f32)).astype(bf16)


def first_kernel(edge, index_ref, x_ref, orb_ref, nu_ref, out_ref):
    slot = pl.program_id(0)
    second_at = pl.multiple_of(index_ref[1, slot] * edge, edge)
    third_at = pl.multiple_of(index_ref[2, slot] * edge, edge)
    nu_block = nu_ref[pl.ds(third_at, edge), :]
    orb_block = orb_ref[pl.ds(second_at, edge), :]
    rank = nu_block.shape[1]
    group = 4
    total = jnp.zeros((edge, rank), f32)
    for start in range(0, edge, group):
        x_high, x_low = split_two(x_ref[0, :, start * edge:(start + group) * edge])
        stacked = jnp.concatenate([x_high, x_low], axis=0)
        product = jnp.concatenate(
            [nu_block * orb_block[j:j + 1, :] for j in range(start, start + group)], axis=0
        )
        high, low = split_two(product)
        main = jnp.dot(stacked, high, preferred_element_type=f32)
        rest = jnp.dot(x_high, low, preferred_element_type=f32)
        total += main[:edge] + (main[edge:] + rest)
    out_ref[...] = jnp.where(index_ref[3, slot] > 0, total, 0.0)


def solve_kernel(edge, blocks, at_ref, part_ref, inverse_ref, a_ref, gram_ref, total_ref):
    total_ref[...] = jnp.zeros_like(total_ref)

    def add_block(block, carry):
        rows = pl.ds(pl.multiple_of(at_ref[block] * edge, edge), edge)
        total_ref[rows, :] += part_ref[pl.ds(pl.multiple_of(block * edge, edge), edge), :]
        return carry

    lax.fori_loop(0, blocks, add_block, 0)
    inverse = inverse_ref[...]
    chunk = min(256, total_ref.shape[0])
    gram_ref[...] = jnp.zeros_like(gram_ref)

    def apply(step, carry):
        rows = pl.ds(pl.multiple_of(step * chunk, chunk), chunk)
        solved = jnp.dot(total_ref[rows, :], inverse, precision=highest, preferred_element_type=f32)
        a_ref[rows, :] = solved
        gram_ref[...] += lax.dot_general(
            solved, solved, (((0,), (0,)), ((), ())), precision=highest, preferred_element_type=f32
        )
        return carry

    lax.fori_loop(0, total_ref.shape[0] // chunk, apply, 0)


def second_kernel(edge, index_ref, x_ref, a_ref, nu_ref, e_ref, out_ref):
    slot = pl.program_id(0)
    first_at = pl.multiple_of(index_ref[0, slot] * edge, edge)
    second_at = pl.multiple_of(index_ref[1, slot] * edge, edge)
    third_at = pl.multiple_of(index_ref[2, slot] * edge, edge)
    live = index_ref[3, slot] > 0

    @pl.when(slot == 0)
    def _():
        out_ref[...] = jnp.zeros_like(out_ref)

    nu_block = nu_ref[pl.ds(third_at, edge), :]
    a_high, a_low = split_two(a_ref[pl.ds(first_at, edge), :])
    weights = jnp.concatenate([a_high, a_high, a_low, a_low], axis=0)
    group = 8
    for start in range(0, edge, group):
        x_high, x_low = split_two(x_ref[0, :, start * edge:(start + group) * edge])
        turned = jnp.concatenate([x_high, x_low], axis=0).T
        e = jnp.dot(
            jnp.concatenate([turned, turned], axis=1), weights, preferred_element_type=f32
        )
        e_ref[0, start * edge:(start + group) * edge, :] = e
        sums = jnp.sum(e.reshape(group, edge, e.shape[1]) * nu_block[None], axis=1)
        rows = pl.ds(pl.multiple_of(second_at + start, group), group)
        out_ref[rows, :] += jnp.where(live, sums, 0.0)


def third_kernel(edge, index_ref, e_ref, b_ref, out_ref):
    slot = pl.program_id(0)
    second_at = pl.multiple_of(index_ref[1, slot] * edge, edge)
    third_at = pl.multiple_of(index_ref[2, slot] * edge, edge)

    @pl.when(slot == 0)
    def _():
        out_ref[...] = jnp.zeros_like(out_ref)

    b_block = b_ref[pl.ds(second_at, edge), :]
    total = jnp.zeros((edge, b_block.shape[1]), f32)
    for j in range(edge):
        total += e_ref[0, j * edge:(j + 1) * edge, :] * b_block[j:j + 1, :]
    out_ref[pl.ds(third_at, edge), :] += jnp.where(index_ref[3, slot] > 0, total, 0.0)


def eye_mask(n):
    return lax.broadcasted_iota(jnp.int32, (n, n), 0) == lax.broadcasted_iota(jnp.int32, (n, n), 1)


def unit_gram(gram, rows):
    diagonal = jnp.where(eye_mask(gram.shape[0]), gram, 0.0)
    along = jnp.sqrt(jnp.sum(diagonal, axis=0, keepdims=True) / rows + epsilon)
    down = jnp.sqrt(jnp.sum(diagonal, axis=1, keepdims=True) / rows + epsilon)
    return gram / down / along / rows, along


def sweep_inverse(a_ref):
    n = a_ref.shape[0]
    lane = lax.broadcasted_iota(jnp.int32, (PANEL, n), 1)
    row = lax.broadcasted_iota(jnp.int32, (PANEL, n), 0)

    def panel_step(step, carry):
        before = a_ref[:PANEL, :]
        panel = before
        for k in range(0, PANEL, 2):
            first = jnp.broadcast_to(panel[:, k:k + 1], panel.shape)
            second = jnp.broadcast_to(panel[:, k + 1:k + 2], panel.shape)
            at_first, at_second = lane == k, lane == k + 1
            unit_first = jnp.where(at_second[:1], 0.0, panel[k:k + 1, :])
            unit_first = jnp.where(at_first[:1], 1.0, unit_first)
            unit_second = jnp.where(at_first[:1], 0.0, panel[k + 1:k + 2, :])
            unit_second = jnp.where(at_second[:1], 1.0, unit_second)
            inverse = 1.0 / first[k:k + 1, :]
            across = second[k:k + 1, :]
            factor = first[k + 1:k + 2, :] * inverse
            inverse_schur = 1.0 / (second[k + 1:k + 2, :] - factor * across)
            new_second = (unit_second - factor * unit_first) * inverse_schur
            new_first = (unit_first - across * new_second) * inverse
            kept = jnp.where(at_first | at_second, 0.0, panel)
            panel = kept - first * new_first - second * new_second
            panel = jnp.where(row == k, new_first, jnp.where(row == k + 1, new_second, panel))
        own = lane < PANEL
        update = jnp.where(own, -panel, panel)
        w_high, w_middle, w_low = split_three(before)
        z_high, z_middle, z_low = split_three(update)
        left = jnp.concatenate([w_low, w_middle, w_high, w_middle, w_high, w_high], axis=0)
        right = jnp.concatenate([z_high, z_middle, z_low, z_high, z_middle, z_high], axis=0)
        change = lax.dot_general(
            left, right, (((0,), (0,)), ((), ())), preferred_element_type=f32
        )
        others = jnp.where(own[:1], 0.0, a_ref[PANEL:, :]) - change[PANEL:, :]
        a_ref[:n - PANEL, :] = pltpu.roll(others, n - PANEL, 1)
        a_ref[n - PANEL:, :] = pltpu.roll(update, n - PANEL, 1)
        return carry

    lax.fori_loop(0, n // PANEL, panel_step, 0)


def inverse_kernel(left_rows, right_rows, left_ref, right_ref, inverse_ref, scale_ref, a_ref):
    left = left_ref[...]
    if left_rows:
        left, scale_ref[...] = unit_gram(left, left_rows)
    else:
        scale_ref[...] = jnp.ones_like(scale_ref)
    right = right_ref[...]
    if right_rows:
        right, _ = unit_gram(right, right_rows)
    n = left.shape[0]
    a_ref[...] = left * right + jnp.where(eye_mask(n), ridge_weight, 0.0)
    sweep_inverse(a_ref)
    inverse_ref[...] = -a_ref[...]


def inverse_of(left, right, left_rows, right_rows, name):
    n = left.shape[0]
    whole = pl.BlockSpec(memory_space=pltpu.VMEM)
    return pl.pallas_call(
        functools.partial(inverse_kernel, left_rows, right_rows),
        out_shape=(jax.ShapeDtypeStruct((n, n), f32), jax.ShapeDtypeStruct((1, n), f32)),
        in_specs=[whole, whole],
        out_specs=(whole, whole),
        scratch_shapes=[pltpu.VMEM((n, n), f32)],
        compiler_params=pltpu.CompilerParams(vmem_limit_bytes=16 << 20),
        cost_estimate=pl.CostEstimate(flops=10**9, bytes_accessed=4 * n * n * 4, transcendentals=0),
        name=name,
    )(left, right)


def per_device(tiles, tile_list, orb_factor, nu_factor):
    slots, edge = tiles.shape[0], tiles.shape[1]
    rank = nu_factor.shape[1]
    first_rows = P_SIZE // lax.axis_size("aux")
    orb_rows = orb_factor.shape[0]
    orb_size = lax.axis_size("orb")
    tile_width = tiles.shape[2]
    index = tile_list - jnp.stack(
        [
            lax.axis_index("aux") * (first_rows // edge),
            lax.axis_index("orb") * (orb_rows // edge),
            jnp.int32(0),
            jnp.int32(0),
        ]
    ).astype(jnp.int32)[:, None]
    tile_spec = pl.BlockSpec((1, edge, tile_width), lambda s, i: (s, 0, 0))

    def full(rows):
        return pl.BlockSpec((rows, rank), lambda s, i: (0, 0))

    own_row = lax.broadcasted_iota(jnp.int32, (orb_size, slots), 0) == lax.axis_index("orb")
    own_at = jnp.where(own_row, index[0].astype(f32)[None], 0.0)
    s_nu = gram_of(nu_factor) / NU
    table = jnp.pad(own_at, ((0, -orb_size % 32), (0, rank - slots)))
    joined = all_reduce(
        jnp.concatenate([gram_of(orb_factor), table], axis=0), ("orb",), 5, "sum_gram_orb"
    )
    s_orb = joined[:rank] / MU
    slot_at = joined[rank:rank + orb_size, :slots].astype(jnp.int32).reshape(-1)

    parts = pl.pallas_call(
        functools.partial(first_kernel, edge),
        out_shape=jax.ShapeDtypeStruct((slots * edge, rank), f32),
        grid_spec=pltpu.PrefetchScalarGridSpec(
            num_scalar_prefetch=1,
            grid=(slots,),
            in_specs=[tile_spec, full(orb_rows), full(nu_factor.shape[0])],
            out_specs=pl.BlockSpec((edge, rank), lambda s, i: (s, 0)),
        ),
        name="mode_first",
    )(index, tiles, orb_factor, nu_factor)
    gathered = lax.all_gather(parts, "orb", axis=0, tiled=True)
    inverse_first, _ = inverse_of(s_orb, s_nu, 0, 0, "inverse_first")
    blocks = slots * orb_size
    vmem = pl.BlockSpec(memory_space=pltpu.VMEM)
    a_new, gram_a = pl.pallas_call(
        functools.partial(solve_kernel, edge, blocks),
        out_shape=(
            jax.ShapeDtypeStruct((first_rows, rank), f32),
            jax.ShapeDtypeStruct((rank, rank), f32),
        ),
        in_specs=[pl.BlockSpec(memory_space=pltpu.SMEM), vmem, vmem],
        out_specs=(vmem, vmem),
        scratch_shapes=[pltpu.VMEM((first_rows, rank), f32)],
        name="solve_first",
    )(slot_at, gathered, inverse_first)
    gram_a = all_reduce(gram_a, ("aux",), 1, "sum_gram_first")

    e_all, partial_second = pl.pallas_call(
        functools.partial(second_kernel, edge),
        out_shape=(
            jax.ShapeDtypeStruct((slots, tile_width, rank), f32),
            jax.ShapeDtypeStruct((orb_rows, rank), f32),
        ),
        grid_spec=pltpu.PrefetchScalarGridSpec(
            num_scalar_prefetch=1,
            grid=(slots,),
            in_specs=[tile_spec, full(first_rows), full(nu_factor.shape[0])],
            out_specs=(
                pl.BlockSpec((1, tile_width, rank), lambda s, i: (s, 0, 0)),
                full(orb_rows),
            ),
        ),
        name="mode_second",
    )(index, tiles, a_new, nu_factor)
    sums_first = jnp.sum(jnp.where(eye_mask(rank), gram_a, 0.0), axis=0)
    scale_first = jnp.sqrt(sums_first / P_SIZE + epsilon)
    second_sums = all_reduce(partial_second / scale_first, ("aux",), 2, "sum_second")
    inverse_second, _ = inverse_of(gram_a, s_nu, P_SIZE, 0, "inverse_second")
    aux_factor = a_new / scale_first
    b_new = jnp.dot(second_sums, inverse_second, precision=highest, preferred_element_type=f32)
    gram_b = all_reduce(gram_of(b_new), ("orb",), 3, "sum_gram_second")

    partial_third = pl.pallas_call(
        functools.partial(third_kernel, edge),
        out_shape=jax.ShapeDtypeStruct((nu_factor.shape[0], rank), f32),
        grid_spec=pltpu.PrefetchScalarGridSpec(
            num_scalar_prefetch=1,
            grid=(slots,),
            in_specs=[
                pl.BlockSpec((1, tile_width, rank), lambda s, i: (s, 0, 0)),
                full(orb_rows),
            ],
            out_specs=full(nu_factor.shape[0]),
        ),
        name="mode_third",
    )(index, e_all, b_new)
    third_sums = all_reduce(partial_third, ("aux", "orb"), 4, "sum_third")
    inverse_third, scale_second = inverse_of(gram_b, gram_a, MU, P_SIZE, "inverse_third")
    orb_updated = b_new / scale_second
    c_new = jnp.dot(
        third_sums / scale_first / scale_second,
        inverse_third,
        precision=highest,
        preferred_element_type=f32,
    )
    scale_third = jnp.sqrt(jnp.sum(c_new * c_new, axis=0) / NU + epsilon)
    nu_updated = c_new / scale_third
    return (aux_factor, orb_updated, nu_updated)


def solution(mesh):
    return jax.shard_map(
        per_device,
        mesh=mesh,
        in_specs=(P(("aux", "orb"), None, None), P(None, ("aux", "orb")), P("orb", None), P()),
        out_specs=(P("aux", None), P("orb", None), P()),
        check_vma=False,
    )
```

profile of v0, /device:TPU:0, one launch (start us, length us, event | category | flops | bytes accessed | tf_op | source)
XLA Modules:
  0.0 289.6 jit_solution(8064999332475309350)
XLA Ops:
  7.2 0.0 all-gather.2.cloned.1.call-start
  7.2 0.1 pad_add_fusion
  7.3 1.3 broadcast_subtract_fusion.index_ref
  8.6 0.0 copy-start.5
  8.6 12.5 %mode_first.1 = f32[512,256]{1,0:T(8,128)} custom-call(s32[4,8]{1,0:T(4,128)} %broadcast_subtract_fusion.index_ref, f32[8,64,4096]{2,1,0:T(8,128)} %x_ref.3, f32[1024,256]{1,0:T(8,128)} %orb_ref.1, f32[512,256]{1,0:T(8,128)} %nu_ref.3), custom_call_target="tpu_custom_call" | custom-call | tf_op jit(solution)/shard_map/mode_first/pallas_call | solution.py:322
  21.2 0.0 all-gather.2.cloned.1.call-update
  21.2 0.0 copy-start.6
  21.2 0.7 convert_bitcast_fusion
  21.9 0.1 broadcast_select_fusion
  22.0 0.0 copy-done.5
  22.0 1.8 fusion.4
  23.9 0.7 select_maximum_fusion.x_ref
  24.6 42.9 %sum_gram_orb.1 = f32[288,256]{1,0:T(8,128)} custom-call(f32[288,256]{1,0:T(8,128)} %select_maximum_fusion.x_ref), custom_call_target="tpu_custom_call" | custom-call | tf_op jit(solution)/shard_map/sum_gram_orb/pallas_call | solution.py:90
  67.5 0.7 slice_convert_fusion
  68.2 0.6 reshape.20.at_ref
  68.8 1.0 slice_multiply_fusion.left_ref
  69.7 0.0 copy-done.6
  69.7 1.0 convolution_multiply_fusion.right_ref
  70.8 16.7 %inverse_first.1 = (f32[256,256]{1,0:T(8,128)S(1)}, f32[1,256]{1,0:T(1,128)}) custom-call(f32[256,256]{1,0:T(8,128)S(1)} %slice_multiply_fusion.left_ref, f32[256,256]{1,0:T(8,128)S(1)} %convolution_multiply_fusion.right_ref), custom_call_target="tpu_custom_call" | custom-call | flops 1000000000 | bytes 1048576 | tf_op jit(solution)/shard_map/inverse_first/pallas_call | solution.py:280
  87.5 0.0 copy-start.2
  87.5 0.7 copy-done.2
  88.2 0.0 all-gather.2.cloned.1.call-done.part_ref
  88.2 11.9 %solve_first.1 = (f32[2048,256]{1,0:T(8,128)}, f32[256,256]{1,0:T(8,128)}) custom-call(s32[32]{0:T(128)} %reshape.20.at_ref, f32[2048,256]{1,0:T(8,128)} %all-gather.2.cloned.1.call-done.part_ref, f32[256,256]{1,0:T(8,128)} %copy-done.2), custom_call_target="tpu_custom_call" | custom-call | tf_op jit(solution)/shard_map/solve_first/pallas_call | solution.py:337
  100.2 20.0 %sum_gram_first.1.left_ref.right_ref = f32[256,256]{1,0:T(8,128)} custom-call(f32[256,256]{1,0:T(8,128)} %get-tuple-element.13.x_ref), custom_call_target="tpu_custom_call" | custom-call | tf_op jit(solution)/shard_map/sum_gram_first/pallas_call | solution.py:90
  120.2 1.0 select_reduce_fusion
  121.2 0.0 copy-start
  121.2 0.9 copy-done
  122.1 16.9 %inverse_second.1 = (f32[256,256]{1,0:T(8,128)S(1)}, f32[1,256]{1,0:T(1,128)}) custom-call(f32[256,256]{1,0:T(8,128)S(1)} %copy-done, f32[256,256]{1,0:T(8,128)S(1)} %convolution_multiply_fusion.right_ref), custom_call_target="tpu_custom_call" | custom-call | flops 1000000000 | bytes 1048576 | tf_op jit(solution)/shard_map/inverse_second/pallas_call | solution.py:280
  139.0 16.9 %mode_second.1 = (f32[8,4096,256]{2,1,0:T(8,128)}, f32[1024,256]{1,0:T(8,128)}) custom-call(s32[4,8]{1,0:T(4,128)} %broadcast_subtract_fusion.index_ref, f32[8,64,4096]{2,1,0:T(8,128)} %x_ref.3, f32[2048,256]{1,0:T(8,128)} %get-tuple-element.12.a_ref, f32[512,256]{1,0:T(8,128)} %nu_ref.3), custom_call_target="tpu_custom_call" | custom-call | tf_op jit(solution)/shard_map/mode_second/pallas_call | solution.py:350
  156.0 2.3 broadcast_divide_fusion.2.x_ref
  158.2 28.6 %sum_second.1 = f32[1024,256]{1,0:T(8,128)} custom-call(f32[1024,256]{1,0:T(8,128)} %broadcast_divide_fusion.2.x_ref), custom_call_target="tpu_custom_call" | custom-call | tf_op jit(solution)/shard_map/sum_second/pallas_call | solution.py:90
  186.9 0.0 copy-start.1
  186.9 2.3 fusion.5.b_ref
  189.2 0.0 copy-start.4
  189.2 2.5 fusion.6.x_ref
  191.7 21.0 %sum_gram_second.1.left_ref = f32[256,256]{1,0:T(8,128)} custom-call(f32[256,256]{1,0:T(8,128)} %fusion.6.x_ref), custom_call_target="tpu_custom_call" | custom-call | tf_op jit(solution)/shard_map/sum_gram_second/pallas_call | solution.py:90
  212.7 0.0 copy-done.1
  212.7 0.0 copy-start.3
  212.7 0.9 copy-done.3
  213.7 0.0 copy-start.7
  213.7 16.5 %inverse_third.1 = (f32[256,256]{1,0:T(8,128)S(1)}, f32[1,256]{1,0:T(1,128)S(1)}) custom-call(f32[256,256]{1,0:T(8,128)S(1)} %copy-done.3, f32[256,256]{1,0:T(8,128)S(1)} %copy-done.1), custom_call_target="tpu_custom_call" | custom-call | flops 1000000000 | bytes 1048576 | tf_op jit(solution)/shard_map/inverse_third/pallas_call | solution.py:280
  230.2 0.0 copy-done.4
  230.2 1.0 broadcast_divide_fusion.1
  231.2 0.0 copy-done.7
  231.2 1.5 broadcast_divide_fusion
  232.7 14.1 %mode_third.1.x_ref = f32[512,256]{1,0:T(8,128)} custom-call(s32[4,8]{1,0:T(4,128)} %broadcast_subtract_fusion.index_ref, f32[8,4096,256]{2,1,0:T(8,128)} %get-tuple-element.17.e_ref, f32[1024,256]{1,0:T(8,128)} %copy-done.4), custom_call_target="tpu_custom_call" | custom-call | tf_op jit(solution)/shard_map/mode_third/pallas_call | solution.py:375
  246.8 33.4 %sum_third.1 = f32[512,256]{1,0:T(8,128)} custom-call(f32[512,256]{1,0:T(8,128)} %mode_third.1.x_ref), custom_call_target="tpu_custom_call" | custom-call | tf_op jit(solution)/shard_map/sum_third/pallas_call | solution.py:90
  280.2 1.6 multiply_reduce_fusion
  281.9 0.8 broadcast_divide_fusion.3
  (5 shorter events, 0.0 us)
Async XLA Ops:
  7.2 81.1 %all-gather.2.cloned.1.call-start = ((), (), s32[]{:S(2)}) async-start(), calls=%async_computation | async-start | bytes 2621440 | tf_op jit(solution)/shard_map/all_gather | solution.py:333
  8.6 13.4 %copy-start.5 = (f32[1024,256]{1,0:T(8,128)S(1)}, f32[1024,256]{1,0:T(8,128)}, u32[]{:S(2)}) copy-start(f32[1024,256]{1,0:T(8,128)} %orb_ref.1) | copy-start | bytes 3145732
  21.2 48.5 %copy-start.6 = (f32[512,256]{1,0:T(8,128)S(1)}, f32[512,256]{1,0:T(8,128)}, u32[]{:S(2)}) copy-start(f32[512,256]{1,0:T(8,128)} %nu_ref.3) | copy-start | bytes 1572868
  87.5 0.7 copy-start.2
  121.2 0.9 copy-start
  186.9 25.8 %copy-start.1 = (f32[256,256]{1,0:T(8,128)S(1)}, f32[256,256]{1,0:T(8,128)}, u32[]{:S(2)}) copy-start(f32[256,256]{1,0:T(8,128)} %sum_gram_first.1.left_ref.right_ref) | copy-start | bytes 786436
  189.2 41.0 %copy-start.4 = (f32[1024,256]{1,0:T(8,128)}, f32[1024,256]{1,0:T(8,128)S(1)}, u32[]{:S(2)}) copy-start(f32[1024,256]{1,0:T(8,128)S(1)} %fusion.5.b_ref) | copy-start | bytes 3145732
  212.7 1.0 copy-start.3
  213.7 17.6 %copy-start.7 = (f32[2048,256]{1,0:T(8,128)S(1)}, f32[2048,256]{1,0:T(8,128)}, u32[]{:S(2)}) copy-start(f32[2048,256]{1,0:T(8,128)} %get-tuple-element.12.a_ref) | copy-start | bytes 6291460
Sparse Core Ops, SparseCore 0:
  21.3 54.4 all-gather.1
where the time goes:
time: 291 us; the launch traced here: 290 us
  Pallas kernels  252 us (87%)
  between operations  14.2 us (5%)
  other arithmetic  11.2 us (4%)
  matrix products  9.29 us (3%)
  local copies, waits for them, and re-layouts  3.2 us (1%)
    pallas_call x5, Pallas kernels, all_reduce(): pl.pallas_call(functools.partial(reduce_kernel, tuple(steps)), out_shape=...  146 us
    pallas_call x3, Pallas kernels, inverse_of(): pl.pallas_call(functools.partial(inverse_kernel, left_rows, right_rows),...  50.1 us
    pallas_call x1, Pallas kernels, per_device(): pl.pallas_call(functools.partial(second_kernel, edge), out_shape=(jax.Sha...  16.9 us
    pallas_call x1, Pallas kernels, per_device(): pl.pallas_call(functools.partial(third_kernel, edge), out_shape=jax.Shape...  14.1 us
    pallas_call x1, Pallas kernels, per_device(): pl.pallas_call(functools.partial(first_kernel, edge), out_shape=jax.Shape...  12.5 us
    pallas_call x1, Pallas kernels, per_device(): pl.pallas_call(functools.partial(solve_kernel, edge, blocks), out_shape=(...  11.9 us
  transfers between devices with their start and end apart: 1, of which 0 were waited for; matrix products, arithmetic and copies ran while one was open for 2% of the time, Pallas kernels for 21%

commit v1 on v0

--- a/solution.py
+++ b/solution.py
@@ -116,51 +116,302 @@
     return high, middle, (rest - middle.astype(f32)).astype(bf16)
 
 
-def first_kernel(edge, index_ref, x_ref, orb_ref, nu_ref, out_ref):
-    slot = pl.program_id(0)
-    second_at = pl.multiple_of(index_ref[1, slot] * edge, edge)
-    third_at = pl.multiple_of(index_ref[2, slot] * edge, edge)
-    nu_block = nu_ref[pl.ds(third_at, edge), :]
-    orb_block = orb_ref[pl.ds(second_at, edge), :]
-    rank = nu_block.shape[1]
-    group = 4
-    total = jnp.zeros((edge, rank), f32)
-    for start in range(0, edge, group):
-        x_high, x_low = split_two(x_ref[0, :, start * edge:(start + group) * edge])
-        stacked = jnp.concatenate([x_high, x_low], axis=0)
-        product = jnp.concatenate(
-            [nu_block * orb_block[j:j + 1, :] for j in range(start, start + group)], axis=0
+def aligned(value, step):
+    return pl.multiple_of(value, step)
+
+
+def dot_t(left, right):
+    return lax.dot_general(left, right, (((0,), (0,)), ((), ())), preferred_element_type=f32)
+
+
+def dot_exact(left, right):
+    l_high, l_middle, l_low = left
+    r_high, r_middle, r_low = right
+    dot = functools.partial(jnp.dot, preferred_element_type=f32)
+    small = dot(l_low, r_high) + dot(l_high, r_low) + dot(l_middle, r_middle)
+    return dot(l_high, r_high) + (dot(l_middle, r_high) + dot(l_high, r_middle) + small)
+
+
+def gram_add(x, even_ref, odd_ref):
+    high, middle, low = split_three(x)
+    pair = jnp.concatenate([high, middle], axis=0)
+    even_ref[...] += dot_t(pair, pair)
+    odd_ref[...] += dot_t(
+        jnp.concatenate([high, high], axis=0), jnp.concatenate([middle, low], axis=0)
+    )
+
+
+def gram_rows(x_ref, even_ref, odd_ref):
+    even_ref[...] = jnp.zeros_like(even_ref)
+    odd_ref[...] = jnp.zeros_like(odd_ref)
+    group = min(4, x_ref.shape[0])
+
+    def step(at, carry):
+        rows = x_ref[pl.ds(at * group, group)]
+        gram_add(rows.reshape(-1, rows.shape[2]), even_ref, odd_ref)
+        return carry
+
+    lax.fori_loop(0, x_ref.shape[0] // group, step, 0)
+    odd = odd_ref[...]
+    return even_ref[...] + (odd + odd.T)
+
+
+def enter(axes):
+    barrier = pltpu.get_barrier_semaphore()
+    count = 0
+    for axis in axes:
+        size, here = lax.axis_size(axis), lax.axis_index(axis)
+        for step in range(1, size):
+            pl.semaphore_signal(
+                barrier, inc=1, device_id={axis: (here + step) % size}, device_id_type=MESH
+            )
+            count += 1
+    pl.semaphore_wait(barrier, count)
+
+
+class Net:
+    def __init__(self, send, recv):
+        self.send, self.recv, self.copies = send, recv, []
+
+    def copy(self, src, dst, to):
+        at = len(self.copies)
+        copy = pltpu.make_async_remote_copy(
+            src_ref=src,
+            dst_ref=dst,
+            send_sem=self.send.at[at],
+            recv_sem=self.recv.at[at],
+            device_id=to,
+            device_id_type=MESH,
         )
-        high, low = split_two(product)
-        main = jnp.dot(stacked, high, preferred_element_type=f32)
-        rest = jnp.dot(x_high, low, preferred_element_type=f32)
-        total += main[:edge] + (main[edge:] + rest)
-    out_ref[...] = jnp.where(index_ref[3, slot] > 0, total, 0.0)
-
-
-def solve_kernel(edge, blocks, at_ref, part_ref, inverse_ref, a_ref, gram_ref, total_ref):
+        copy.start()
+        self.copies.append(copy)
+        return copy
+
+    def scatter(self, axis, src, land):
+        size, here = lax.axis_size(axis), lax.axis_index(axis)
+        rows = land.shape[1]
+        land[here] = src[pl.ds(aligned(here * rows, 8), rows), :]
+        copies = []
+        for step in range(1, size):
+            to = (here + step) % size
+            block = src.at[pl.ds(aligned(to * rows, 8), rows), :]
+            copies.append(self.copy(block, land.at[here], {axis: to}))
+        return copies
+
+    def share(self, axis, src, land):
+        size, here = lax.axis_size(axis), lax.axis_index(axis)
+        land[here] = src[...]
+        return [
+            self.copy(src, land.at[here], {axis: (here + step) % size}) for step in range(1, size)
+        ]
+
+    def spread(self, axis, full, rows):
+        size, here = lax.axis_size(axis), lax.axis_index(axis)
+        own = full.at[pl.ds(aligned(here * rows, 8), rows), :]
+        return [self.copy(own, own, {axis: (here + step) % size}) for step in range(1, size)]
+
+    def finish(self):
+        for copy in self.copies:
+            copy.wait_send()
+
+
+def arrive(copies):
+    for copy in copies:
+        copy.wait_recv()
+
+
+def total_of(land):
+    total = land[0]
+    for at in range(1, land.shape[0]):
+        total += land[at]
+    return total
+
+
+def first_kernel(
+    edge, list_ref, x_hbm, orb_ref, nu_ref, parts_out, table_out, inverse_out, s_nu_out,
+    x_buf, parts, table, even, odd, gram, gram_land, work, x_sem, send, recv, hop_send, hop_recv
+):
+    slots = list_ref.shape[1]
+    here, size = lax.axis_index("orb"), lax.axis_size("orb")
+    mine = lax.axis_index("aux")
+    rank = nu_ref.shape[2]
+    orb_rows = orb_ref.shape[0] * edge
+    first_base = mine * (P_SIZE // lax.axis_size("aux") // edge)
+    gram_rows_each = gram_land.shape[1]
+
+    def load(slot):
+        return pltpu.make_async_copy(x_hbm.at[slot], x_buf.at[slot], x_sem.at[slot])
+
+    for slot in range(slots):
+        load(slot).start()
+    enter(("aux", "orb"))
+    net = Net(send, recv)
+
+    def hop(way, distance, slot):
+        at = ((here - way * distance) * slots + slot) * edge
+        rows = parts.at[pl.ds(aligned(at, edge), edge), :]
+        lane = 0 if way > 0 else 1
+        return pltpu.make_async_remote_copy(
+            src_ref=rows,
+            dst_ref=rows,
+            send_sem=hop_send.at[lane, distance, slot],
+            recv_sem=hop_recv.at[lane, distance, slot],
+            device_id={"orb": here + way},
+            device_id_type=MESH,
+        )
+
+    def landed(way, distance, slot):
+        at = ((here - way * distance) * slots + slot) * edge
+        rows = parts.at[pl.ds(aligned(at, edge), edge), :]
+        lane = 0 if way > 0 else 1
+        return pltpu.make_async_remote_copy(
+            src_ref=rows,
+            dst_ref=rows,
+            send_sem=hop_send.at[lane, distance - 1, slot],
+            recv_sem=hop_recv.at[lane, distance - 1, slot],
+            device_id={"orb": here - way},
+            device_id_type=MESH,
+        )
+
+    def goes(way, distance):
+        at = here if way > 0 else size - 1 - here
+        return (at + size - 1 - distance) // (size - 1) * ((2 * size - 3 - at) // (size - 1)) > 0
+
+    def ends(way, distance):
+        return here == size - 1 if way > 0 else here == 0
+
+    def forward(distance, slot):
+        for way in (1, -1):
+
+            @pl.when(goes(way, distance))
+            def _():
+                landed(way, distance, slot).wait_recv()
+                hop(way, distance, slot).start()
+
+    def slot_step(slot, carry):
+        load(slot).wait()
+        nu_block = nu_ref[list_ref[2, slot]]
+        orb_block = orb_ref[lax.rem(list_ref[1, slot], orb_ref.shape[0])]
+        group = 4
+        total = jnp.zeros((edge, rank), f32)
+        for start in range(0, edge, group):
+            x_high, x_low = split_two(x_buf[slot, :, start * edge:(start + group) * edge])
+            stacked = jnp.concatenate([x_high, x_low], axis=0)
+            product = jnp.concatenate(
+                [nu_block * orb_block[j:j + 1, :] for j in range(start, start + group)], axis=0
+            )
+            high, low = split_two(product)
+            main = jnp.dot(stacked, high, preferred_element_type=f32)
+            rest = jnp.dot(x_high, low, preferred_element_type=f32)
+            total += main[:edge] + (main[edge:] + rest)
+        live = list_ref[3, slot].astype(f32)
+        parts[pl.ds(aligned((here * slots + slot) * edge, edge), edge), :] = total * live
+        for way in (1, -1):
+
+            @pl.when(goes(way, 0))
+            def _():
+                hop(way, 0, slot).start()
+
+        return carry
+
+    early, late = slots // 4, slots - slots // 4
+    lax.fori_loop(0, early, slot_step, 0)
+
+    row = lax.broadcasted_iota(jnp.int32, (slots, table.shape[1]), 0)
+    own_at = jnp.zeros((slots, table.shape[1]), f32)
+    for slot in range(slots):
+        value = (list_ref[0, slot] - first_base).astype(f32)
+        own_at = jnp.where(row == slot, value, own_at)
+    table[pl.ds(aligned(here * slots, 8), slots), :] = own_at
+    table_copies = net.spread("orb", table, slots)
+    gram[...] = gram_rows(orb_ref, even, odd)
+    gram_copies = []
+    for step in range(1, size):
+        block = gram.at[pl.ds(aligned(mine * gram_rows_each, 8), gram_rows_each), :]
+        gram_copies.append(net.copy(block, gram_land.at[here], {"orb": (here + step) % size}))
+    gram_land[here] = gram[pl.ds(aligned(mine * gram_rows_each, 8), gram_rows_each), :]
+    s_nu = gram_rows(nu_ref, even, odd) / NU
+    s_nu_out[...] = s_nu
+    lax.fori_loop(early, late, slot_step, 0)
+    arrive(gram_copies)
+    work[pl.ds(aligned(mine * gram_rows_each, 8), gram_rows_each), :] = total_of(gram_land)
+    share_copies = net.spread("aux", work, gram_rows_each)
+    lax.fori_loop(late, slots, slot_step, 0)
+
+    if size > 2:
+
+        def near(slot, carry):
+            forward(1, slot)
+            return carry
+
+        lax.fori_loop(0, slots, near, 0)
+    arrive(share_copies)
+    even[...] = work[...] / (orb_rows * size) * s_nu_out[...] + jnp.where(
+        eye_mask(rank), ridge_weight, 0.0
+    )
+
+    def beside(step):
+        if size > 3:
+            forward(2, step)
+
+    sweep_inverse(even, beside if rank // PANEL == slots else None)
+    inverse_out[...] = -even[...]
+    far = 2 if rank // PANEL != slots else 3
+    for distance in range(far, size - 1):
+
+        def pass_on(slot, carry, distance=distance):
+            forward(distance, slot)
+            return carry
+
+        lax.fori_loop(0, slots, pass_on, 0)
+
+    def last(slot, carry):
+        for way in (1, -1):
+            for distance in range(1, size):
+
+                @pl.when(ends(way, distance))
+                def _():
+                    landed(way, distance, slot).wait_recv()
+
+            for distance in range(size - 1):
+
+                @pl.when(goes(way, distance))
+                def _():
+                    hop(way, distance, slot).wait_send()
+
+        return carry
+
+    lax.fori_loop(0, slots, last, 0)
+    arrive(table_copies)
+    net.finish()
+    parts_out[...] = parts[...]
+    table_out[...] = table[...].astype(jnp.int32)
+
+
+def solve_kernel(edge, blocks, at_ref, part_ref, inverse_ref, a_ref, gram_ref, total_ref, even, odd):
     total_ref[...] = jnp.zeros_like(total_ref)
 
     def add_block(block, carry):
-        rows = pl.ds(pl.multiple_of(at_ref[block] * edge, edge), edge)
-        total_ref[rows, :] += part_ref[pl.ds(pl.multiple_of(block * edge, edge), edge), :]
+        rows = pl.ds(aligned(at_ref[block, 0] * edge, edge), edge)
+        total_ref[rows, :] += part_ref[pl.ds(aligned(block * edge, edge), edge), :]
         return carry
 
     lax.fori_loop(0, blocks, add_block, 0)
-    inverse = inverse_ref[...]
-    chunk = min(256, total_ref.shape[0])
-    gram_ref[...] = jnp.zeros_like(gram_ref)
+    inverse = split_three(inverse_ref[...])
+    even[...] = jnp.zeros_like(even)
+    odd[...] = jnp.zeros_like(odd)
+    chunk = min(512, total_ref.shape[0])
 
     def apply(step, carry):
-        rows = pl.ds(pl.multiple_of(step * chunk, chunk), chunk)
-        solved = jnp.dot(total_ref[rows, :], inverse, precision=highest, preferred_element_type=f32)
+        rows = pl.ds(aligned(step * chunk, chunk), chunk)
+        solved = dot_exact(split_three(total_ref[rows, :]), inverse)
         a_ref[rows, :] = solved
-        gram_ref[...] += lax.dot_general(
-            solved, solved, (((0,), (0,)), ((), ())), precision=highest, preferred_element_type=f32
-        )
+        gram_add(solved, even, odd)
         return carry
 
     lax.fori_loop(0, total_ref.shape[0] // chunk, apply, 0)
+    cross = odd[...]
+    gram_ref[...] = even[...] + (cross + cross.T)
 
 
 def second_kernel(edge, index_ref, x_ref, a_ref, nu_ref, e_ref, out_ref):
@@ -217,12 +468,14 @@
     return gram / down / along / rows, along
 
 
-def sweep_inverse(a_ref):
+def sweep_inverse(a_ref, beside=None):
     n = a_ref.shape[0]
     lane = lax.broadcasted_iota(jnp.int32, (PANEL, n), 1)
     row = lax.broadcasted_iota(jnp.int32, (PANEL, n), 0)
 
     def panel_step(step, carry):
+        if beside is not None:
+            beside(step)
         before = a_ref[:PANEL, :]
         panel = before
         for k in range(0, PANEL, 2):
@@ -309,31 +562,46 @@
     def full(rows):
         return pl.BlockSpec((rows, rank), lambda s, i: (0, 0))
 
-    own_row = lax.broadcasted_iota(jnp.int32, (orb_size, slots), 0) == lax.axis_index("orb")
-    own_at = jnp.where(own_row, index[0].astype(f32)[None], 0.0)
-    s_nu = gram_of(nu_factor) / NU
-    table = jnp.pad(own_at, ((0, -orb_size % 32), (0, rank - slots)))
-    joined = all_reduce(
-        jnp.concatenate([gram_of(orb_factor), table], axis=0), ("orb",), 5, "sum_gram_orb"
-    )
-    s_orb = joined[:rank] / MU
-    slot_at = joined[rank:rank + orb_size, :slots].astype(jnp.int32).reshape(-1)
-
-    parts = pl.pallas_call(
+    aux_size = lax.axis_size("aux")
+    vmem = pl.BlockSpec(memory_space=pltpu.VMEM)
+    blocks = slots * orb_size
+    square = pltpu.VMEM((rank, rank), f32)
+    net_count = 2 * (orb_size - 1) + aux_size - 1
+    parts, table, inverse_first, s_nu = pl.pallas_call(
         functools.partial(first_kernel, edge),
-        out_shape=jax.ShapeDtypeStruct((slots * edge, rank), f32),
-        grid_spec=pltpu.PrefetchScalarGridSpec(
-            num_scalar_prefetch=1,
-            grid=(slots,),
-            in_specs=[tile_spec, full(orb_rows), full(nu_factor.shape[0])],
-            out_specs=pl.BlockSpec((edge, rank), lambda s, i: (s, 0)),
+        out_shape=(
+            jax.ShapeDtypeStruct((blocks * edge, rank), f32),
+            jax.ShapeDtypeStruct((blocks, 128), jnp.int32),
+            jax.ShapeDtypeStruct((rank, rank), f32),
+            jax.ShapeDtypeStruct((rank, rank), f32),
         ),
-        name="mode_first",
-    )(index, tiles, orb_factor, nu_factor)
-    gathered = lax.all_gather(parts, "orb", axis=0, tiled=True)
-    inverse_first, _ = inverse_of(s_orb, s_nu, 0, 0, "inverse_first")
-    blocks = slots * orb_size
-    vmem = pl.BlockSpec(memory_space=pltpu.VMEM)
+        in_specs=[
+            pl.BlockSpec(memory_space=pltpu.SMEM),
+            pl.BlockSpec(memory_space=pltpu.HBM),
+            vmem,
+            vmem,
+        ],
+        out_specs=(vmem, vmem, vmem, vmem),
+        scratch_shapes=[
+            pltpu.VMEM((slots, edge, tile_width), f32),
+            pltpu.VMEM((blocks * edge, rank), f32),
+            pltpu.VMEM((blocks, 128), f32),
+            square,
+            square,
+            square,
+            pltpu.VMEM((orb_size, rank // aux_size, rank), f32),
+            square,
+            pltpu.SemaphoreType.DMA((slots,)),
+            pltpu.SemaphoreType.DMA((net_count,)),
+            pltpu.SemaphoreType.DMA((net_count,)),
+            pltpu.SemaphoreType.DMA((2, orb_size - 1, slots)),
+            pltpu.SemaphoreType.DMA((2, orb_size - 1, slots)),
+        ],
+        compiler_params=pltpu.CompilerParams(
+            collective_id=5, has_side_effects=True, vmem_limit_bytes=32 << 20
+        ),
+        name="first_gather",
+    )(tile_list, tiles, orb_factor.reshape(-1, edge, rank), nu_factor.reshape(-1, edge, rank))
     a_new, gram_a = pl.pallas_call(
         functools.partial(solve_kernel, edge, blocks),
         out_shape=(
@@ -342,9 +610,9 @@
         ),
         in_specs=[pl.BlockSpec(memory_space=pltpu.SMEM), vmem, vmem],
         out_specs=(vmem, vmem),
-        scratch_shapes=[pltpu.VMEM((first_rows, rank), f32)],
+        scratch_shapes=[pltpu.VMEM((first_rows, rank), f32), square, square],
         name="solve_first",
-    )(slot_at, gathered, inverse_first)
+    )(table, parts, inverse_first)
     gram_a = all_reduce(gram_a, ("aux",), 1, "sum_gram_first")
 
     e_all, partial_second = pl.pallas_call(

time: 291 us -> 244 us (0.84)
  Pallas kernels: 252 us -> 220 us
  between operations: 14.2 us -> 0.79 us
  local copies, waits for them, and re-layouts: 3.2 us -> 9.91 us
  matrix products: 9.29 us -> 5.24 us
  other arithmetic: 11.2 us -> 7.41 us
    pallas_call x5 -> x4, Pallas kernels: 146 us -> 101 us  [all_reduce(): pl.pallas_call(functools.partial(reduce_kernel, tuple(steps)), out_shape=...]
    pallas_call x1, Pallas kernels: 12.5 us -> 46.3 us  [per_device(): pl.pallas_call(functools.partial(first_kernel, edge), out_shape=(jax.Shap...]
    pallas_call x3 -> x2, Pallas kernels: 50.1 us -> 33.4 us  [inverse_of(): pl.pallas_call(functools.partial(inverse_kernel, left_rows, right_rows),...]
    unnamed x16 -> x28, local copies, waits for them, and re-layouts: 2.61 us -> 9.91 us
    pallas_call x1, Pallas kernels: 11.9 us -> 8.95 us  [per_device(): pl.pallas_call(functools.partial(solve_kernel, edge, blocks), out_shape=(...]
  transfers between devices with their start and end apart: 1 -> 0, of which waited for: 0 -> 0; matrix products, arithmetic and copies ran while one was open for 2% -> 0% of each run, Pallas kernels for 21% -> 0%
where the time goes in v1:
time: 244 us
  Pallas kernels  220 us (90%)
  local copies, waits for them, and re-layouts  9.91 us (4%)
  other arithmetic  7.41 us (3%)
  matrix products  5.24 us (2%)
    pallas_call x4, Pallas kernels, all_reduce(): pl.pallas_call(functools.partial(reduce_kernel, tuple(steps)), out_shape=...  101 us
    pallas_call x1, Pallas kernels, per_device(): pl.pallas_call(functools.partial(first_kernel, edge), out_shape=(jax.Shap...  46.3 us
    pallas_call x2, Pallas kernels, inverse_of(): pl.pallas_call(functools.partial(inverse_kernel, left_rows, right_rows),...  33.4 us
    pallas_call x1, Pallas kernels, per_device(): pl.pallas_call(functools.partial(second_kernel, edge), out_shape=(jax.Sha...  16.9 us
    pallas_call x1, Pallas kernels, per_device(): pl.pallas_call(functools.partial(third_kernel, edge), out_shape=jax.Shape...  14.1 us
    unnamed x28, local copies, waits for them, and re-layouts  9.91 us
    pallas_call x1, Pallas kernels, per_device(): pl.pallas_call(functools.partial(solve_kernel, edge, blocks), out_shape=(...  8.95 us

profile of v1, /device:TPU:0, one launch (start us, length us, event | category | flops | bytes accessed | tf_op | source)
XLA Modules:
  0.0 243.6 jit_solution(11126837122693203411)
XLA Ops:
  0.6 0.0 copy-start
  0.6 3.4 %copy-done = f32[8,64,4096]{2,1,0:T(8,128)S(1)} copy-done((f32[8,64,4096]{2,1,0:T(8,128)S(1)}, f32[8,64,4096]{2,1,0:T(8,128)}, u32[]{:S(2)}) %copy-start) | copy-done | bytes 8388632
  4.0 0.0 copy-start.2
  4.0 1.0 copy-done.2
  5.1 0.0 copy-start.4
  5.1 1.2 copy-done.4
  6.3 0.0 copy-start.8
  6.3 0.7 copy-done.8
  7.0 46.3 %first_gather.1 = (f32[2048,256]{1,0:T(8,128)S(1)}, s32[32,128]{1,0:T(8,128)S(1)}, f32[256,256]{1,0:T(8,128)S(1)}, f32[256,256]{1,0:T(8,128)S(1)}) custom-call(s32[4,8]{1,0:T(4,128)S(1)} %copy-done.8, f32[8,64,4096]{2,1,0:T(8,128)S(1)} %copy-done, f32[16,64,256]{2,1,0:T(8,128)S(1)} %bitcast.11, f32[8,64,256]{2,1,0:T(8,128)S(1)} %bitcast.10), custom_call_target="tpu_custom_call" | custom-call | tf_op jit(solution)/shard_map/first_gather/pallas_call | solution.py:570
  53.3 0.0 copy-start.1
  53.3 1.3 copy-done.1
  54.6 0.0 copy-start.5
  54.6 0.7 copy-done.5
  55.3 0.0 copy-start.7
  55.3 0.6 copy-done.7
  55.9 0.0 copy-start.9
  55.9 9.0 %solve_first.1 = (f32[2048,256]{1,0:T(8,128)}, f32[256,256]{1,0:T(8,128)}) custom-call(s32[32,128]{1,0:T(8,128)} %copy-done.7, f32[2048,256]{1,0:T(8,128)} %copy-done.1, f32[256,256]{1,0:T(8,128)} %copy-done.5), custom_call_target="tpu_custom_call" | custom-call | tf_op jit(solution)/shard_map/solve_first/pallas_call | solution.py:605
  64.9 0.1 pad_add_fusion
  65.0 0.0 copy-done.9
  65.0 0.6 broadcast_subtract_fusion.index_ref
  65.6 16.9 %mode_second.1 = (f32[8,4096,256]{2,1,0:T(8,128)}, f32[1024,256]{1,0:T(8,128)}) custom-call(s32[4,8]{1,0:T(4,128)} %broadcast_subtract_fusion.index_ref, f32[8,64,4096]{2,1,0:T(8,128)} %x_ref.1, f32[2048,256]{1,0:T(8,128)} %get-tuple-element.17.a_ref, f32[512,256]{1,0:T(8,128)} %nu_ref.1), custom_call_target="tpu_custom_call" | custom-call | tf_op jit(solution)/shard_map/mode_second/pallas_call | solution.py:618
  82.5 17.7 %sum_gram_first.1.left_ref.right_ref = f32[256,256]{1,0:T(8,128)} custom-call(f32[256,256]{1,0:T(8,128)} %get-tuple-element.18.x_ref), custom_call_target="tpu_custom_call" | custom-call | tf_op jit(solution)/shard_map/sum_gram_first/pallas_call | solution.py:90
  100.2 1.0 select_reduce_fusion
  101.2 0.0 copy-start.3
  101.2 2.3 broadcast_divide_fusion.2.x_ref
  103.5 29.2 %sum_second.1 = f32[1024,256]{1,0:T(8,128)} custom-call(f32[1024,256]{1,0:T(8,128)} %broadcast_divide_fusion.2.x_ref), custom_call_target="tpu_custom_call" | custom-call | tf_op jit(solution)/shard_map/sum_second/pallas_call | solution.py:90
  132.7 0.0 copy-start.13
  132.8 0.0 copy-done.3
  132.8 16.9 %inverse_second.1 = (f32[256,256]{1,0:T(8,128)S(1)}, f32[1,256]{1,0:T(1,128)}) custom-call(f32[256,256]{1,0:T(8,128)S(1)} %copy-done.3, f32[256,256]{1,0:T(8,128)S(1)} %get-tuple-element.20.right_ref), custom_call_target="tpu_custom_call" | custom-call | flops 1000000000 | bytes 1048576 | tf_op jit(solution)/shard_map/inverse_second/pallas_call | solution.py:533
  149.6 0.0 copy-done.13
  149.7 1.0 fusion.4.b_ref
  150.7 0.0 copy-start.10
  150.7 2.6 %fusion.5.x_ref = f32[256,256]{1,0:T(8,128)} fusion(f32[1024,256]{1,0:T(8,128)S(1)} %fusion.4.b_ref), kind=kOutput, calls=%fused_computation.16 | convolution fusion | flops 805306368 | bytes 1310720 | tf_op jit(solution)/shard_map/dot_general | solution.py:104
  153.3 19.0 %sum_gram_second.1.left_ref = f32[256,256]{1,0:T(8,128)} custom-call(f32[256,256]{1,0:T(8,128)} %fusion.5.x_ref), custom_call_target="tpu_custom_call" | custom-call | tf_op jit(solution)/shard_map/sum_gram_second/pallas_call | solution.py:90
  172.3 0.0 copy-start.6
  172.3 0.9 copy-done.6
  173.2 16.5 %inverse_third.1 = (f32[256,256]{1,0:T(8,128)S(1)}, f32[1,256]{1,0:T(1,128)S(1)}) custom-call(f32[256,256]{1,0:T(8,128)S(1)} %copy-done.6, f32[256,256]{1,0:T(8,128)S(1)} %copy-done.3), custom_call_target="tpu_custom_call" | custom-call | flops 1000000000 | bytes 1048576 | tf_op jit(solution)/shard_map/inverse_third/pallas_call | solution.py:533
  189.7 0.0 copy-done.10
  189.7 14.1 %mode_third.1.x_ref = f32[512,256]{1,0:T(8,128)} custom-call(s32[4,8]{1,0:T(4,128)} %broadcast_subtract_fusion.index_ref, f32[8,4096,256]{2,1,0:T(8,128)} %get-tuple-element.23.e_ref, f32[1024,256]{1,0:T(8,128)} %copy-done.10), custom_call_target="tpu_custom_call" | custom-call | tf_op jit(solution)/shard_map/mode_third/pallas_call | solution.py:643
  203.8 0.0 copy-start.11
  203.8 34.7 %sum_third.1 = f32[512,256]{1,0:T(8,128)} custom-call(f32[512,256]{1,0:T(8,128)} %mode_third.1.x_ref), custom_call_target="tpu_custom_call" | custom-call | tf_op jit(solution)/shard_map/sum_third/pallas_call | solution.py:90
  238.5 1.6 multiply_reduce_fusion
  240.2 0.0 copy-start.12
  240.2 0.8 broadcast_divide_fusion.3
  241.0 0.0 copy-done.11
  241.0 1.0 broadcast_divide_fusion.1
  242.1 0.0 copy-done.12
  242.1 1.5 broadcast_divide_fusion
  (4 shorter events, 0.0 us)
Async XLA Ops:
  0.6 3.4 %copy-start = (f32[8,64,4096]{2,1,0:T(8,128)S(1)}, f32[8,64,4096]{2,1,0:T(8,128)}, u32[]{:S(2)}) copy-start(f32[8,64,4096]{2,1,0:T(8,128)} %x_ref.1) | copy-start | bytes 25165828
  4.0 1.0 copy-start.2
  5.1 1.2 copy-start.4
  6.3 0.7 copy-start.8
  53.3 1.3 copy-start.1
  54.6 0.7 copy-start.5
  55.3 0.6 copy-start.7
  55.9 9.0 %copy-start.9 = (s32[4,8]{1,0:T(4,128)S(1)}, s32[4,8]{1,0:T(4,128)}, u32[]{:S(2)}) copy-start(s32[4,8]{1,0:T(4,128)} %list_ref.1) | copy-start | bytes 388
  101.2 31.5 %copy-start.3 = (f32[256,256]{1,0:T(8,128)S(1)}, f32[256,256]{1,0:T(8,128)}, u32[]{:S(2)}) copy-start(f32[256,256]{1,0:T(8,128)} %sum_gram_first.1.left_ref.right_ref) | copy-start | bytes 786436
  132.7 16.9 %copy-start.13 = (f32[1024,256]{1,0:T(8,128)S(1)}, f32[1024,256]{1,0:T(8,128)}, u32[]{:S(2)}) copy-start(f32[1024,256]{1,0:T(8,128)} %sum_second.1) | copy-start | bytes 3145732
  150.7 39.0 %copy-start.10 = (f32[1024,256]{1,0:T(8,128)}, f32[1024,256]{1,0:T(8,128)S(1)}, u32[]{:S(2)}) copy-start(f32[1024,256]{1,0:T(8,128)S(1)} %fusion.4.b_ref) | copy-start | bytes 3145732
  172.3 1.0 copy-start.6
  203.8 37.2 %copy-start.11 = (f32[1024,256]{1,0:T(8,128)S(1)}, f32[1024,256]{1,0:T(8,128)}, u32[]{:S(2)}) copy-start(f32[1024,256]{1,0:T(8,128)} %copy-done.10) | copy-start | bytes 3145732
  240.2 1.9 copy-start.12

commit v2 on v1

--- a/solution.py
+++ b/solution.py
@@ -20,88 +20,6 @@
 
 
 MESH = pl.DeviceIdType.MESH
-
-
-def reduce_kernel(steps, x_ref, out_ref, sum_ref, all_ref, *scratch):
-    count = len(steps)
-    landing = scratch[:count]
-    send_sem, recv_sem = scratch[count:]
-    bits, partners = [], []
-    for axis, bit in steps:
-        here = lax.axis_index(axis)
-        value = (here // (1 << bit)) % 2
-        bits.append(value)
-        partners.append({axis: here + (1 - 2 * value) * (1 << bit)})
-    barrier = pltpu.get_barrier_semaphore()
-    for partner in partners:
-        pl.semaphore_signal(barrier, inc=1, device_id=partner, device_id_type=MESH)
-    pl.semaphore_wait(barrier, count)
-    sum_ref[...] = x_ref[...]
-    length = sum_ref.shape[0]
-    start = jnp.int32(0)
-    kept = []
-    for step in range(count):
-        length //= 2
-        mine = pl.multiple_of(start + bits[step] * length, 8)
-        other = pl.multiple_of(start + (1 - bits[step]) * length, 8)
-        copy = pltpu.make_async_remote_copy(
-            src_ref=sum_ref.at[pl.ds(other, length), :],
-            dst_ref=landing[step],
-            send_sem=send_sem.at[step],
-            recv_sem=recv_sem.at[step],
-            device_id=partners[step],
-            device_id_type=MESH,
-        )
-        copy.start()
-        copy.wait()
-        sum_ref[pl.ds(mine, length), :] += landing[step][...]
-        start = mine
-        kept.append((mine, length))
-    mine, length = kept[-1]
-    all_ref[pl.ds(mine, length), :] = sum_ref[pl.ds(mine, length), :]
-    for step in reversed(range(count)):
-        mine, length = kept[step]
-        rows = all_ref.at[pl.ds(mine, length), :]
-        copy = pltpu.make_async_remote_copy(
-            src_ref=rows,
-            dst_ref=rows,
-            send_sem=send_sem.at[count + step],
-            recv_sem=recv_sem.at[count + step],
-            device_id=partners[step],
-            device_id_type=MESH,
-        )
-        copy.start()
-        copy.wait()
-    out_ref[...] = all_ref[...]
-
-
-def all_reduce(x, axes, number, name):
-    steps = []
-    for axis in axes:
-        size = lax.axis_size(axis)
-        if size & (size - 1):
-            return lax.psum(x, axes)
-        steps += [(axis, bit) for bit in range(size.bit_length() - 1)]
-    rows, columns = x.shape
-    if rows % (8 << len(steps)):
-        return lax.psum(x, axes)
-    count = len(steps)
-    vmem = pl.BlockSpec(memory_space=pltpu.VMEM)
-    return pl.pallas_call(
-        functools.partial(reduce_kernel, tuple(steps)),
-        out_shape=jax.ShapeDtypeStruct(x.shape, f32),
-        in_specs=[vmem],
-        out_specs=vmem,
-        scratch_shapes=[pltpu.VMEM((rows, columns), f32)] * 2
-        + [pltpu.VMEM((rows >> (step + 1), columns), f32) for step in range(count)]
-        + [pltpu.SemaphoreType.DMA((2 * count,)), pltpu.SemaphoreType.DMA((2 * count,))],
-        compiler_params=pltpu.CompilerParams(collective_id=number, has_side_effects=True),
-        name=name,
-    )(x)
-
-
-def gram_of(matrix):
-    return jnp.dot(matrix.T, matrix, precision=highest, preferred_element_type=f32)
 
 
 def split_two(x):
@@ -414,49 +332,6 @@
     gram_ref[...] = even[...] + (cross + cross.T)
 
 
-def second_kernel(edge, index_ref, x_ref, a_ref, nu_ref, e_ref, out_ref):
-    slot = pl.program_id(0)
-    first_at = pl.multiple_of(index_ref[0, slot] * edge, edge)
-    second_at = pl.multiple_of(index_ref[1, slot] * edge, edge)
-    third_at = pl.multiple_of(index_ref[2, slot] * edge, edge)
-    live = index_ref[3, slot] > 0
-
-    @pl.when(slot == 0)
-    def _():
-        out_ref[...] = jnp.zeros_like(out_ref)
-
-    nu_block = nu_ref[pl.ds(third_at, edge), :]
-    a_high, a_low = split_two(a_ref[pl.ds(first_at, edge), :])
-    weights = jnp.concatenate([a_high, a_high, a_low, a_low], axis=0)
-    group = 8
-    for start in range(0, edge, group):
-        x_high, x_low = split_two(x_ref[0, :, start * edge:(start + group) * edge])
-        turned = jnp.concatenate([x_high, x_low], axis=0).T
-        e = jnp.dot(
-            jnp.concatenate([turned, turned], axis=1), weights, preferred_element_type=f32
-        )
-        e_ref[0, start * edge:(start + group) * edge, :] = e
-        sums = jnp.sum(e.reshape(group, edge, e.shape[1]) * nu_block[None], axis=1)
-        rows = pl.ds(pl.multiple_of(second_at + start, group), group)
-        out_ref[rows, :] += jnp.where(live, sums, 0.0)
-
-
-def third_kernel(edge, index_ref, e_ref, b_ref, out_ref):
-    slot = pl.program_id(0)
-    second_at = pl.multiple_of(index_ref[1, slot] * edge, edge)
-    third_at = pl.multiple_of(index_ref[2, slot] * edge, edge)
-
-    @pl.when(slot == 0)
-    def _():
-        out_ref[...] = jnp.zeros_like(out_ref)
-
-    b_block = b_ref[pl.ds(second_at, edge), :]
-    total = jnp.zeros((edge, b_block.shape[1]), f32)
-    for j in range(edge):
-        total += e_ref[0, j * edge:(j + 1) * edge, :] * b_block[j:j + 1, :]
-    out_ref[pl.ds(third_at, edge), :] += jnp.where(index_ref[3, slot] > 0, total, 0.0)
-
-
 def eye_mask(n):
     return lax.broadcasted_iota(jnp.int32, (n, n), 0) == lax.broadcasted_iota(jnp.int32, (n, n), 1)
 
@@ -468,7 +343,7 @@
     return gram / down / along / rows, along
 
 
-def sweep_inverse(a_ref, beside=None):
+def sweep_inverse(a_ref, beside=None, first=0, last=None):
     n = a_ref.shape[0]
     lane = lax.broadcasted_iota(jnp.int32, (PANEL, n), 1)
     row = lax.broadcasted_iota(jnp.int32, (PANEL, n), 0)
@@ -509,37 +384,126 @@
         a_ref[n - PANEL:, :] = pltpu.roll(update, n - PANEL, 1)
         return carry
 
-    lax.fori_loop(0, n // PANEL, panel_step, 0)
-
-
-def inverse_kernel(left_rows, right_rows, left_ref, right_ref, inverse_ref, scale_ref, a_ref):
-    left = left_ref[...]
-    if left_rows:
-        left, scale_ref[...] = unit_gram(left, left_rows)
-    else:
-        scale_ref[...] = jnp.ones_like(scale_ref)
-    right = right_ref[...]
-    if right_rows:
-        right, _ = unit_gram(right, right_rows)
-    n = left.shape[0]
-    a_ref[...] = left * right + jnp.where(eye_mask(n), ridge_weight, 0.0)
-    sweep_inverse(a_ref)
-    inverse_ref[...] = -a_ref[...]
-
-
-def inverse_of(left, right, left_rows, right_rows, name):
-    n = left.shape[0]
-    whole = pl.BlockSpec(memory_space=pltpu.VMEM)
-    return pl.pallas_call(
-        functools.partial(inverse_kernel, left_rows, right_rows),
-        out_shape=(jax.ShapeDtypeStruct((n, n), f32), jax.ShapeDtypeStruct((1, n), f32)),
-        in_specs=[whole, whole],
-        out_specs=(whole, whole),
-        scratch_shapes=[pltpu.VMEM((n, n), f32)],
-        compiler_params=pltpu.CompilerParams(vmem_limit_bytes=16 << 20),
-        cost_estimate=pl.CostEstimate(flops=10**9, bytes_accessed=4 * n * n * 4, transcendentals=0),
-        name=name,
-    )(left, right)
+    lax.fori_loop(first, n // PANEL if last is None else last, panel_step, 0)
+
+
+def sweep_kernel(
+    edge, list_ref, x_hbm, nu_ref, a_ref, gram_ref, s_nu_ref, b_out, c_out, scale_out,
+    x_buf, e_ref, part, work, even, odd, gram_land, gram_a, terms, terms_land, b_full, b_blocks,
+    gram_b, z_land, gram_sum, thirds, thirds_land, thirds_z, third_sums, x_sem, send, recv
+):
+    slots = list_ref.shape[1]
+    here, size = lax.axis_index("orb"), lax.axis_size("orb")
+    mine, count = lax.axis_index("aux"), lax.axis_size("aux")
+    rank = nu_ref.shape[2]
+    orb_rows, nu_rows = b_full.shape[0], third_sums.shape[0]
+    half = slots // 2
+
+    def load(slot):
+        return pltpu.make_async_copy(x_hbm.at[slot], x_buf.at[slot], x_sem.at[slot])
+
+    for slot in range(slots):
+        load(slot).start()
+    enter(("aux", "orb"))
+    net = Net(send, recv)
+    gram_copies = net.scatter("aux", gram_ref, gram_land)
+
+    def rows_of(ref):
+        return pl.ds(aligned(mine * (ref.shape[0] // count), 8), ref.shape[0] // count)
+
+    def second_step(slot, carry):
+        load(slot).wait()
+        nu_block = nu_ref[list_ref[2, slot]]
+        a_high, a_low = split_two(a_ref[lax.rem(list_ref[0, slot], a_ref.shape[0])])
+        weights = jnp.concatenate([a_high, a_high, a_low, a_low], axis=0)
+        group = 8
+        for start in range(0, edge, group):
+            x_high, x_low = split_two(x_buf[slot, :, start * edge:(start + group) * edge])
+            turned = jnp.concatenate([x_high, x_low], axis=0).T
+            e = jnp.dot(
+                jnp.concatenate([turned, turned], axis=1), weights, preferred_element_type=f32
+            )
+            e_ref[slot, start * edge:(start + group) * edge, :] = e
+            part[slot, start:start + group, :] = jnp.sum(
+                e.reshape(group, edge, rank) * nu_block[None], axis=1
+            )
+        return carry
+
+    def gather_blocks(dimension, out_ref):
+        blocks = out_ref.shape[0] // edge
+        places = [lax.rem(list_ref[dimension, slot], blocks) for slot in range(slots)]
+        lives = [list_ref[3, slot].astype(f32) for slot in range(slots)]
+
+        def block_step(block, carry):
+            total = jnp.zeros((edge, rank), f32)
+            for slot in range(slots):
+                weight = (places[slot] == block).astype(f32) * lives[slot]
+                total += part[slot] * weight
+            out_ref[pl.ds(aligned(block * edge, edge), edge), :] = total
+            return carry
+
+        lax.fori_loop(0, blocks, block_step, 0)
+
+    lax.fori_loop(0, half, second_step, 0)
+    arrive(gram_copies)
+    gram_a[rows_of(gram_a), :] = total_of(gram_land)
+    gram_copies = net.spread("aux", gram_a, rank // count)
+    lax.fori_loop(half, slots, second_step, 0)
+    gather_blocks(1, terms)
+    terms_copies = net.scatter("aux", terms, terms_land)
+
+    arrive(gram_copies)
+    unit_a, scale_a = unit_gram(gram_a[...], P_SIZE)
+    ridge = jnp.where(eye_mask(rank), ridge_weight, 0.0)
+    work[...] = unit_a * s_nu_ref[...] + ridge
+    sweep_inverse(work)
+    inverse = split_three(-work[...])
+    arrive(terms_copies)
+    b_own = dot_exact(split_three(total_of(terms_land) / scale_a), inverse)
+    b_full[rows_of(b_full), :] = b_own
+    b_copies = net.spread("aux", b_full, orb_rows // count)
+    scale_out[...] = jnp.broadcast_to(scale_a, scale_out.shape)
+    arrive(b_copies)
+    b_blocks[...] = b_full[...].reshape(b_blocks.shape)
+    gram_b[...] = gram_rows(b_blocks, even, odd)
+    z_copies = net.share("orb", gram_b.at[rows_of(gram_b), :], z_land)
+
+    def third_step(slot, carry):
+        b_block = b_blocks[lax.rem(list_ref[1, slot], b_blocks.shape[0])]
+        total = jnp.zeros((edge, rank), f32)
+        for j in range(edge):
+            total += e_ref[slot, j * edge:(j + 1) * edge, :] * b_block[j:j + 1, :]
+        part[slot] = total
+        return carry
+
+    lax.fori_loop(0, half, third_step, 0)
+    arrive(z_copies)
+    gram_sum[rows_of(gram_sum), :] = total_of(z_land)
+    gram_copies = net.spread("aux", gram_sum, rank // count)
+    lax.fori_loop(half, slots, third_step, 0)
+    gather_blocks(2, thirds)
+    third_copies = net.scatter("aux", thirds, thirds_land)
+
+    arrive(gram_copies)
+    unit_b, scale_b = unit_gram(gram_sum[...], orb_rows * size)
+    work[...] = unit_b * unit_gram(gram_a[...], P_SIZE)[0] + ridge
+    panels = rank // PANEL
+    sweep_inverse(work, None, 0, panels // 2)
+    arrive(third_copies)
+    thirds_land[mine] = total_of(thirds_land)
+    third_copies = net.share("orb", thirds_land.at[mine], thirds_z)
+    sweep_inverse(work, None, panels // 2, panels - 1)
+    arrive(third_copies)
+    third_sums[rows_of(third_sums), :] = total_of(thirds_z)
+    third_copies = net.spread("aux", third_sums, nu_rows // count)
+    sweep_inverse(work, None, panels - 1, panels)
+    inverse = split_three(-work[...])
+    b_out[...] = b_full[...] / scale_b
+    arrive(third_copies)
+    c_new = dot_exact(split_three(third_sums[...] / scale_a / scale_b), inverse)
+    scale_c = jnp.sqrt(jnp.sum(c_new * c_new, axis=0, keepdims=True) / nu_rows + epsilon)
+    c_out[...] = c_new / scale_c
+    net.finish()
 
 
 def per_device(tiles, tile_list, orb_factor, nu_factor):
@@ -549,19 +513,6 @@
     orb_rows = orb_factor.shape[0]
     orb_size = lax.axis_size("orb")
     tile_width = tiles.shape[2]
-    index = tile_list - jnp.stack(
-        [
-            lax.axis_index("aux") * (first_rows // edge),
-            lax.axis_index("orb") * (orb_rows // edge),
-            jnp.int32(0),
-            jnp.int32(0),
-        ]
-    ).astype(jnp.int32)[:, None]
-    tile_spec = pl.BlockSpec((1, edge, tile_width), lambda s, i: (s, 0, 0))
-
-    def full(rows):
-        return pl.BlockSpec((rows, rank), lambda s, i: (0, 0))
-
     aux_size = lax.axis_size("aux")
     vmem = pl.BlockSpec(memory_space=pltpu.VMEM)
     blocks = slots * orb_size
@@ -598,7 +549,7 @@
             pltpu.SemaphoreType.DMA((2, orb_size - 1, slots)),
         ],
         compiler_params=pltpu.CompilerParams(
-            collective_id=5, has_side_effects=True, vmem_limit_bytes=32 << 20
+            collective_id=5, has_side_effects=True, vmem_limit_bytes=60 << 20
         ),
         name="first_gather",
     )(tile_list, tiles, orb_factor.reshape(-1, edge, rank), nu_factor.reshape(-1, edge, rank))
@@ -611,61 +562,69 @@
         in_specs=[pl.BlockSpec(memory_space=pltpu.SMEM), vmem, vmem],
         out_specs=(vmem, vmem),
         scratch_shapes=[pltpu.VMEM((first_rows, rank), f32), square, square],
+        compiler_params=pltpu.CompilerParams(vmem_limit_bytes=60 << 20),
         name="solve_first",
     )(table, parts, inverse_first)
-    gram_a = all_reduce(gram_a, ("aux",), 1, "sum_gram_first")
-
-    e_all, partial_second = pl.pallas_call(
-        functools.partial(second_kernel, edge),
+    orb_blocks = orb_rows // edge
+    nu_rows = nu_factor.shape[0]
+    net_count = 7 * (aux_size - 1) + 2 * (orb_size - 1)
+
+    def room(*shape):
+        return pltpu.VMEM(shape, f32)
+
+    orb_updated, nu_updated, scale = pl.pallas_call(
+        functools.partial(sweep_kernel, edge),
         out_shape=(
-            jax.ShapeDtypeStruct((slots, tile_width, rank), f32),
             jax.ShapeDtypeStruct((orb_rows, rank), f32),
+            jax.ShapeDtypeStruct((nu_rows, rank), f32),
+            jax.ShapeDtypeStruct((8, rank), f32),
         ),
-        grid_spec=pltpu.PrefetchScalarGridSpec(
-            num_scalar_prefetch=1,
-            grid=(slots,),
-            in_specs=[tile_spec, full(first_rows), full(nu_factor.shape[0])],
-            out_specs=(
-                pl.BlockSpec((1, tile_width, rank), lambda s, i: (s, 0, 0)),
-                full(orb_rows),
-            ),
+        in_specs=[
+            pl.BlockSpec(memory_space=pltpu.SMEM),
+            pl.BlockSpec(memory_space=pltpu.HBM),
+            vmem,
+            vmem,
+            vmem,
+            vmem,
+        ],
+        out_specs=(vmem, vmem, vmem),
+        scratch_shapes=[
+            room(slots, edge, tile_width),
+            room(slots, tile_width, rank),
+            room(slots, edge, rank),
+            square,
+            square,
+            square,
+            room(aux_size, rank // aux_size, rank),
+            square,
+            room(orb_rows, rank),
+            room(aux_size, orb_rows // aux_size, rank),
+            room(orb_rows, rank),
+            room(orb_blocks, edge, rank),
+            square,
+            room(orb_size, rank // aux_size, rank),
+            square,
+            room(nu_rows, rank),
+            room(aux_size, nu_rows // aux_size, rank),
+            room(orb_size, nu_rows // aux_size, rank),
+            room(nu_rows, rank),
+            pltpu.SemaphoreType.DMA((slots,)),
+            pltpu.SemaphoreType.DMA((net_count,)),
+            pltpu.SemaphoreType.DMA((net_count,)),
+        ],
+        compiler_params=pltpu.CompilerParams(
+            collective_id=6, has_side_effects=True, vmem_limit_bytes=60 << 20
         ),
-        name="mode_second",
-    )(index, tiles, a_new, nu_factor)
-    sums_first = jnp.sum(jnp.where(eye_mask(rank), gram_a, 0.0), axis=0)
-    scale_first = jnp.sqrt(sums_first / P_SIZE + epsilon)
-    second_sums = all_reduce(partial_second / scale_first, ("aux",), 2, "sum_second")
-    inverse_second, _ = inverse_of(gram_a, s_nu, P_SIZE, 0, "inverse_second")
-    aux_factor = a_new / scale_first
-    b_new = jnp.dot(second_sums, inverse_second, precision=highest, preferred_element_type=f32)
-    gram_b = all_reduce(gram_of(b_new), ("orb",), 3, "sum_gram_second")
-
-    partial_third = pl.pallas_call(
-        functools.partial(third_kernel, edge),
-        out_shape=jax.ShapeDtypeStruct((nu_factor.shape[0], rank), f32),
-        grid_spec=pltpu.PrefetchScalarGridSpec(
-            num_scalar_prefetch=1,
-            grid=(slots,),
-            in_specs=[
-                pl.BlockSpec((1, tile_width, rank), lambda s, i: (s, 0, 0)),
-                full(orb_rows),
-            ],
-            out_specs=full(nu_factor.shape[0]),
-        ),
-        name="mode_third",
-    )(index, e_all, b_new)
-    third_sums = all_reduce(partial_third, ("aux", "orb"), 4, "sum_third")
-    inverse_third, scale_second = inverse_of(gram_b, gram_a, MU, P_SIZE, "inverse_third")
-    orb_updated = b_new / scale_second
-    c_new = jnp.dot(
-        third_sums / scale_first / scale_second,
-        inverse_third,
-        precision=highest,
-        preferred_element_type=f32,
+        name="second_third",
+    )(
+        tile_list,
+        tiles,
+        nu_factor.reshape(-1, edge, rank),
+        a_new.reshape(-1, edge, rank),
+        gram_a,
+        s_nu,
     )
-    scale_third = jnp.sqrt(jnp.sum(c_new * c_new, axis=0) / NU + epsilon)
-    nu_updated = c_new / scale_third
-    return (aux_factor, orb_updated, nu_updated)
+    return (a_new / scale[:1], orb_updated, nu_updated)
 
 
 def solution(mesh):

time: 244 us -> 139 us (0.57)
  Pallas kernels: 220 us -> 134 us
  local copies, waits for them, and re-layouts: 9.91 us -> 3.03 us
  other arithmetic: 7.41 us -> 1.46 us
  matrix products: 5.24 us -> 0 us
    pallas_call x8 -> x1, Pallas kernels: 165 us -> 76.7 us  [per_device(): pl.pallas_call(functools.partial(sweep_kernel, edge), out_shape=(jax.Shap...]
    unnamed x28 -> x8, local copies, waits for them, and re-layouts: 9.91 us -> 2.33 us
    dot_general x3 -> x0, matrix products: 5.24 us -> none  [the longest x1 2.6 us: gram_of(): jnp.dot(matrix.T, matrix, precision=highest, preferred_element_type=f32)]
    div x4 -> x1, other arithmetic: 5.66 us -> 1.46 us  [per_device(): return (a_new / scale[:1], orb_updated, nu_updated)]
where the time goes in v2:
time: 139 us
  Pallas kernels  134 us (96%)
  local copies, waits for them, and re-layouts  3.03 us (2%)
  other arithmetic  1.46 us (1%)
    pallas_call x1, Pallas kernels, per_device(): pl.pallas_call(functools.partial(sweep_kernel, edge), out_shape=(jax.Shap...  76.7 us
    pallas_call x1, Pallas kernels, per_device(): pl.pallas_call(functools.partial(first_kernel, edge), out_shape=(jax.Shap...  48 us
    pallas_call x1, Pallas kernels, per_device(): pl.pallas_call(functools.partial(solve_kernel, edge, blocks), out_shape=(...  8.94 us

profile of v2, /device:TPU:0, one launch (start us, length us, event | category | flops | bytes accessed | tf_op | source)
XLA Modules:
  0.0 138.8 jit_solution(14462917780530767175)
XLA Ops:
  0.6 48.0 %first_gather.1 = (f32[2048,256]{1,0:T(8,128)}, s32[32,128]{1,0:T(8,128)}, f32[256,256]{1,0:T(8,128)}, f32[256,256]{1,0:T(8,128)}) custom-call(s32[4,8]{1,0:T(4,128)} %list_ref.3, f32[8,64,4096]{2,1,0:T(8,128)} %x_hbm.3, f32[16,64,256]{2,1,0:T(8,128)} %bitcast.7, f32[8,64,256]{2,1,0:T(8,128)} %bitcast.5), custom_call_target="tpu_custom_call" | custom-call | tf_op jit(solution)/shard_map/first_gather/pallas_call | solution.py:521
  48.6 8.9 %solve_first.1 = (f32[2048,256]{1,0:T(8,128)}, f32[256,256]{1,0:T(8,128)}) custom-call(s32[32,128]{1,0:T(8,128)} %get-tuple-element.12.at_ref, f32[2048,256]{1,0:T(8,128)} %get-tuple-element.13.part_ref, f32[256,256]{1,0:T(8,128)} %get-tuple-element.14.inverse_ref), custom_call_target="tpu_custom_call" | custom-call | tf_op jit(solution)/shard_map/solve_first/pallas_call | solution.py:556
  57.5 0.0 copy-start
  57.5 76.7 %second_third.1 = (f32[1024,256]{1,0:T(8,128)}, f32[512,256]{1,0:T(8,128)}, f32[8,256]{1,0:T(8,128)}) custom-call(s32[4,8]{1,0:T(4,128)} %list_ref.3, f32[8,64,4096]{2,1,0:T(8,128)} %x_hbm.3, f32[8,64,256]{2,1,0:T(8,128)} %bitcast.6, f32[32,64,256]{2,1,0:T(8,128)} %bitcast.4, f32[256,256]{1,0:T(8,128)} %get-tuple-element.16.gram_ref, ...), custom_call_target="tpu_custom_call" | custom-call | tf_op jit(solution)/shard_map/second_third/pallas_call | solution.py:575
  134.3 0.7 slice.3
  135.0 0.0 copy-done
  135.0 0.0 copy-start.1
  135.0 1.5 %broadcast_divide_fusion = f32[2048,256]{1,0:T(8,128)} fusion(f32[2048,256]{1,0:T(8,128)S(1)} %copy-done, f32[256]{0:T(256)S(1)} %bitcast.8), kind=kLoop, calls=%fused_computation | loop fusion | flops 524288 | bytes 4195328 | tf_op jit(solution)/shard_map/div | solution.py:627
  136.5 0.1 copy-done.1
  136.6 0.0 copy-start.2
  136.6 1.0 copy.9
  137.6 0.4 copy-done.2
  138.0 0.8 copy.10
Async XLA Ops:
  57.5 77.5 %copy-start = (f32[2048,256]{1,0:T(8,128)S(1)}, f32[2048,256]{1,0:T(8,128)}, u32[]{:S(2)}) copy-start(f32[2048,256]{1,0:T(8,128)} %get-tuple-element.15) | copy-start | bytes 6291460
  135.0 1.6 %copy-start.1 = (f32[1024,256]{1,0:T(8,128)S(1)}, f32[1024,256]{1,0:T(8,128)}, u32[]{:S(2)}) copy-start(f32[1024,256]{1,0:T(8,128)} %get-tuple-element.25) | copy-start | bytes 3145732
  136.6 1.4 %copy-start.2 = (f32[512,256]{1,0:T(8,128)S(1)}, f32[512,256]{1,0:T(8,128)}, u32[]{:S(2)}) copy-start(f32[512,256]{1,0:T(8,128)} %get-tuple-element.26) | copy-start | bytes 1572868

commit v3 on v2

--- a/solution.py
+++ b/solution.py
@@ -343,33 +343,84 @@
     return gram / down / along / rows, along
 
 
+def pivot_panel(tiles, cols, lane, row):
+    height = len(tiles[0])
+    sub = tiles[0][0].shape[0]
+
+    def columns(first):
+        return [
+            [jnp.broadcast_to(tile[:, k:k + 1], tile.shape) for tile in tiles[0]]
+            for k in range(first, first + cols)
+        ]
+
+    def take(pieces, k):
+        at = k % sub
+        return pieces[k // sub][at:at + 1, :]
+
+    def step(pieces, firsts, seconds, k, new_first, new_second, clear=None):
+        out = []
+        for g in range(height):
+            base = pieces[g] if clear is None else jnp.where(clear, 0.0, pieces[g])
+            value = base - firsts[g] * new_first - seconds[g] * new_second
+            if g == k // sub:
+                value = jnp.where(row == k % sub, new_first, value)
+                value = jnp.where(row == k % sub + 1, new_second, value)
+            out.append(value)
+        return out
+
+    now = columns(0)
+    later = None
+    for start in range(0, height * sub, cols):
+        for j in range(0, cols, 2):
+            k = start + j
+            if j == cols // 2 and start + cols < height * sub:
+                later = columns(start + cols)
+            firsts, seconds = now[j], now[j + 1]
+            a, b = take(firsts, k), take(seconds, k)
+            c, d = take(firsts, k + 1), take(seconds, k + 1)
+            scale = 1.0 / (a * d - b * c)
+            a, b, c, d = d * scale, b * scale, c * scale, a * scale
+            for i in range(j + 2, cols):
+                up, down = take(now[i], k), take(now[i], k + 1)
+                now[i] = step(now[i], firsts, seconds, k, a * up - b * down, d * down - c * up)
+            if later is not None:
+                for i in range(cols):
+                    up, down = take(later[i], k), take(later[i], k + 1)
+                    later[i] = step(
+                        later[i], firsts, seconds, k, a * up - b * down, d * down - c * up
+                    )
+            for h, pieces in enumerate(tiles):
+                up, down = take(pieces, k), take(pieces, k + 1)
+                clear = None
+                if h == 0:
+                    at_up, at_down = lane == k, lane == k + 1
+                    clear = at_up | at_down
+                    up = jnp.where(at_up[:1], 1.0, jnp.where(at_down[:1], 0.0, up))
+                    down = jnp.where(at_down[:1], 1.0, jnp.where(at_up[:1], 0.0, down))
+                tiles[h] = step(
+                    pieces, firsts, seconds, k, a * up - b * down, d * down - c * up, clear
+                )
+        now, later = later, None
+    return tiles
+
+
 def sweep_inverse(a_ref, beside=None, first=0, last=None):
     n = a_ref.shape[0]
+    sub, wide = 8, 128
     lane = lax.broadcasted_iota(jnp.int32, (PANEL, n), 1)
-    row = lax.broadcasted_iota(jnp.int32, (PANEL, n), 0)
+    tile_lane = lax.broadcasted_iota(jnp.int32, (sub, wide), 1)
+    tile_row = lax.broadcasted_iota(jnp.int32, (sub, wide), 0)
 
     def panel_step(step, carry):
         if beside is not None:
             beside(step)
         before = a_ref[:PANEL, :]
-        panel = before
-        for k in range(0, PANEL, 2):
-            first = jnp.broadcast_to(panel[:, k:k + 1], panel.shape)
-            second = jnp.broadcast_to(panel[:, k + 1:k + 2], panel.shape)
-            at_first, at_second = lane == k, lane == k + 1
-            unit_first = jnp.where(at_second[:1], 0.0, panel[k:k + 1, :])
-            unit_first = jnp.where(at_first[:1], 1.0, unit_first)
-            unit_second = jnp.where(at_first[:1], 0.0, panel[k + 1:k + 2, :])
-            unit_second = jnp.where(at_second[:1], 1.0, unit_second)
-            inverse = 1.0 / first[k:k + 1, :]
-            across = second[k:k + 1, :]
-            factor = first[k + 1:k + 2, :] * inverse
-            inverse_schur = 1.0 / (second[k + 1:k + 2, :] - factor * across)
-            new_second = (unit_second - factor * unit_first) * inverse_schur
-            new_first = (unit_first - across * new_second) * inverse
-            kept = jnp.where(at_first | at_second, 0.0, panel)
-            panel = kept - first * new_first - second * new_second
-            panel = jnp.where(row == k, new_first, jnp.where(row == k + 1, new_second, panel))
+        tiles = [
+            [before[g:g + sub, h:h + wide] for g in range(0, PANEL, sub)]
+            for h in range(0, n, wide)
+        ]
+        tiles = pivot_panel(tiles, 8, tile_lane, tile_row)
+        panel = jnp.concatenate([jnp.concatenate(pieces, axis=0) for pieces in tiles], axis=1)
         own = lane < PANEL
         update = jnp.where(own, -panel, panel)
         w_high, w_middle, w_low = split_three(before)
@@ -476,13 +527,12 @@
         part[slot] = total
         return carry
 
-    lax.fori_loop(0, half, third_step, 0)
+    lax.fori_loop(0, slots, third_step, 0)
+    gather_blocks(2, thirds)
+    third_copies = net.scatter("aux", thirds, thirds_land)
     arrive(z_copies)
     gram_sum[rows_of(gram_sum), :] = total_of(z_land)
     gram_copies = net.spread("aux", gram_sum, rank // count)
-    lax.fori_loop(half, slots, third_step, 0)
-    gather_blocks(2, thirds)
-    third_copies = net.scatter("aux", thirds, thirds_land)
 
     arrive(gram_copies)
     unit_b, scale_b = unit_gram(gram_sum[...], orb_rows * size)

time: 139 us -> 134 us (0.964)
  Pallas kernels: 134 us -> 128 us
    pallas_call x1, Pallas kernels: 76.7 us -> 71 us  [per_device(): pl.pallas_call(functools.partial(sweep_kernel, edge), out_shape=(jax.Shap...]
where the time goes in v3:
time: 134 us; the launch traced here: 133 us
  Pallas kernels  128 us (96%)
  local copies, waits for them, and re-layouts  3.03 us (2%)
  other arithmetic  1.46 us (1%)
    pallas_call x1, Pallas kernels, per_device(): pl.pallas_call(functools.partial(sweep_kernel, edge), out_shape=(jax.Shap...  71 us
    pallas_call x1, Pallas kernels, per_device(): pl.pallas_call(functools.partial(first_kernel, edge), out_shape=(jax.Shap...  48 us
    pallas_call x1, Pallas kernels, per_device(): pl.pallas_call(functools.partial(solve_kernel, edge, blocks), out_shape=(...  8.94 us

profile of v3, /device:TPU:0, one launch (start us, length us, event | category | flops | bytes accessed | tf_op | source)
XLA Modules:
  0.0 133.0 jit_solution(2021205152517043424)
XLA Ops:
  0.6 48.0 %first_gather.1 = (f32[2048,256]{1,0:T(8,128)}, s32[32,128]{1,0:T(8,128)}, f32[256,256]{1,0:T(8,128)}, f32[256,256]{1,0:T(8,128)}) custom-call(s32[4,8]{1,0:T(4,128)} %list_ref.3, f32[8,64,4096]{2,1,0:T(8,128)} %x_hbm.3, f32[16,64,256]{2,1,0:T(8,128)} %bitcast.7, f32[8,64,256]{2,1,0:T(8,128)} %bitcast.5), custom_call_target="tpu_custom_call" | custom-call | tf_op jit(solution)/shard_map/first_gather/pallas_call | solution.py:571
  48.6 8.9 %solve_first.1 = (f32[2048,256]{1,0:T(8,128)}, f32[256,256]{1,0:T(8,128)}) custom-call(s32[32,128]{1,0:T(8,128)} %get-tuple-element.12.at_ref, f32[2048,256]{1,0:T(8,128)} %get-tuple-element.13.part_ref, f32[256,256]{1,0:T(8,128)} %get-tuple-element.14.inverse_ref), custom_call_target="tpu_custom_call" | custom-call | tf_op jit(solution)/shard_map/solve_first/pallas_call | solution.py:606
  57.5 0.0 copy-start
  57.5 71.0 %second_third.1 = (f32[1024,256]{1,0:T(8,128)}, f32[512,256]{1,0:T(8,128)}, f32[8,256]{1,0:T(8,128)}) custom-call(s32[4,8]{1,0:T(4,128)} %list_ref.3, f32[8,64,4096]{2,1,0:T(8,128)} %x_hbm.3, f32[8,64,256]{2,1,0:T(8,128)} %bitcast.6, f32[32,64,256]{2,1,0:T(8,128)} %bitcast.4, f32[256,256]{1,0:T(8,128)} %get-tuple-element.16.gram_ref, ...), custom_call_target="tpu_custom_call" | custom-call | tf_op jit(solution)/shard_map/second_third/pallas_call | solution.py:625
  128.5 0.7 slice.3
  129.2 0.0 copy-done
  129.2 0.0 copy-start.1
  129.2 1.5 %broadcast_divide_fusion = f32[2048,256]{1,0:T(8,128)} fusion(f32[2048,256]{1,0:T(8,128)S(1)} %copy-done, f32[256]{0:T(256)S(1)} %bitcast.8), kind=kLoop, calls=%fused_computation | loop fusion | flops 524288 | bytes 4195328 | tf_op jit(solution)/shard_map/div | solution.py:677
  130.7 0.1 copy-done.1
  130.8 0.0 copy-start.2
  130.8 1.0 copy.9
  131.8 0.4 copy-done.2
  132.2 0.8 copy.10
Async XLA Ops:
  57.5 71.7 %copy-start = (f32[2048,256]{1,0:T(8,128)S(1)}, f32[2048,256]{1,0:T(8,128)}, u32[]{:S(2)}) copy-start(f32[2048,256]{1,0:T(8,128)} %get-tuple-element.15) | copy-start | bytes 6291460
  129.2 1.6 %copy-start.1 = (f32[1024,256]{1,0:T(8,128)S(1)}, f32[1024,256]{1,0:T(8,128)}, u32[]{:S(2)}) copy-start(f32[1024,256]{1,0:T(8,128)} %get-tuple-element.25) | copy-start | bytes 3145732
  130.8 1.4 %copy-start.2 = (f32[512,256]{1,0:T(8,128)S(1)}, f32[512,256]{1,0:T(8,128)}, u32[]{:S(2)}) copy-start(f32[512,256]{1,0:T(8,128)} %get-tuple-element.26) | copy-start | bytes 1572868

commit v4 on v3

v4 whole, which is shorter than its diff:
```python
import functools

import jax
import jax.numpy as jnp
from jax import lax
from jax.experimental import pallas as pl
from jax.experimental.pallas import tpu as pltpu
from jax.sharding import PartitionSpec as P

P_SIZE = 16384
MU = 4096
NU = 512

ridge_weight = 0.5
epsilon = 1e-06
highest = lax.Precision.HIGHEST
f32 = jnp.float32
bf16 = jnp.bfloat16
PANEL = 32


MESH = pl.DeviceIdType.MESH


def split_two(x):
    high = x.astype(bf16)
    return high, (x - high.astype(f32)).astype(bf16)


def split_three(x):
    high = x.astype(bf16)
    rest = x - high.astype(f32)
    middle = rest.astype(bf16)
    return high, middle, (rest - middle.astype(f32)).astype(bf16)


def aligned(value, step):
    return pl.multiple_of(value, step)


def dot_t(left, right):
    return lax.dot_general(left, right, (((0,), (0,)), ((), ())), preferred_element_type=f32)


def dot_exact(left, right):
    l_high, l_middle, l_low = left
    r_high, r_middle, r_low = right
    dot = functools.partial(jnp.dot, preferred_element_type=f32)
    small = dot(l_low, r_high) + dot(l_high, r_low) + dot(l_middle, r_middle)
    return dot(l_high, r_high) + (dot(l_middle, r_high) + dot(l_high, r_middle) + small)


def gram_add(x, even_ref, odd_ref):
    high, middle, low = split_three(x)
    pair = jnp.concatenate([high, middle], axis=0)
    even_ref[...] += dot_t(pair, pair)
    odd_ref[...] += dot_t(
        jnp.concatenate([high, high], axis=0), jnp.concatenate([middle, low], axis=0)
    )


def gram_rows(x_ref, even_ref, odd_ref):
    even_ref[...] = jnp.zeros_like(even_ref)
    odd_ref[...] = jnp.zeros_like(odd_ref)
    group = min(4, x_ref.shape[0])

    def step(at, carry):
        rows = x_ref[pl.ds(at * group, group)]
        gram_add(rows.reshape(-1, rows.shape[2]), even_ref, odd_ref)
        return carry

    lax.fori_loop(0, x_ref.shape[0] // group, step, 0)
    odd = odd_ref[...]
    return even_ref[...] + (odd + odd.T)


def enter(axes):
    barrier = pltpu.get_barrier_semaphore()
    count = 0
    for axis in axes:
        size, here = lax.axis_size(axis), lax.axis_index(axis)
        for step in range(1, size):
            pl.semaphore_signal(
                barrier, inc=1, device_id={axis: (here + step) % size}, device_id_type=MESH
            )
            count += 1
    pl.semaphore_wait(barrier, count)


class Net:
    def __init__(self, send, recv):
        self.send, self.recv, self.copies = send, recv, []

    def copy(self, src, dst, to):
        at = len(self.copies)
        copy = pltpu.make_async_remote_copy(
            src_ref=src,
            dst_ref=dst,
            send_sem=self.send.at[at],
            recv_sem=self.recv.at[at],
            device_id=to,
            device_id_type=MESH,
        )
        copy.start()
        self.copies.append(copy)
        return copy

    def scatter(self, axis, src, land):
        size, here = lax.axis_size(axis), lax.axis_index(axis)
        rows = land.shape[1]
        land[here] = src[pl.ds(aligned(here * rows, 8), rows), :]
        copies = []
        for step in range(1, size):
            to = (here + step) % size
            block = src.at[pl.ds(aligned(to * rows, 8), rows), :]
            copies.append(self.copy(block, land.at[here], {axis: to}))
        return copies

    def share(self, axis, src, land):
        size, here = lax.axis_size(axis), lax.axis_index(axis)
        land[here] = src[...]
        return [
            self.copy(src, land.at[here], {axis: (here + step) % size}) for step in range(1, size)
        ]

    def spread(self, axis, full, rows):
        size, here = lax.axis_size(axis), lax.axis_index(axis)
        own = full.at[pl.ds(aligned(here * rows, 8), rows), :]
        return [self.copy(own, own, {axis: (here + step) % size}) for step in range(1, size)]

    def spread_pairs(self, axis, full, rows, landed=None):
        size, here = lax.axis_size(axis), lax.axis_index(axis)
        chips, chip, core = size // 2, here // 2, here % 2
        other = here + 1 - 2 * core

        def block(owner):
            return full.at[pl.ds(aligned(owner * rows, 8), rows), :]

        own = block(here)
        far = [
            self.copy(own, own, {axis: (chip + step) % chips * 2 + core})
            for step in range(1, chips)
        ]
        near = [self.copy(own, own, {axis: other})]
        if landed is not None:
            landed(here)
        for step, copy in enumerate(far, 1):
            source = (chip + chips - step) % chips * 2
            copy.wait_recv()
            near.append(self.copy(block(source + core), block(source + core), {axis: other}))
            if landed is not None:
                landed(source + core)
        for step, copy in enumerate(near):
            copy.wait_recv()
            if landed is not None:
                landed((chip + chips - step) % chips * 2 + 1 - core)

    def finish(self):
        for copy in self.copies:
            copy.wait_send()


def arrive(copies):
    for copy in copies:
        copy.wait_recv()


def total_of(land):
    total = land[0]
    for at in range(1, land.shape[0]):
        total += land[at]
    return total


def eye_mask(n):
    return lax.broadcasted_iota(jnp.int32, (n, n), 0) == lax.broadcasted_iota(jnp.int32, (n, n), 1)


def unit_gram(gram, rows):
    diagonal = jnp.where(eye_mask(gram.shape[0]), gram, 0.0)
    along = jnp.sqrt(jnp.sum(diagonal, axis=0, keepdims=True) / rows + epsilon)
    down = jnp.sqrt(jnp.sum(diagonal, axis=1, keepdims=True) / rows + epsilon)
    return gram / down / along / rows, along


def pivot_panel(tiles, cols, lane, row):
    height = len(tiles[0])
    sub = tiles[0][0].shape[0]

    def columns(first):
        return [
            [jnp.broadcast_to(tile[:, k:k + 1], tile.shape) for tile in tiles[0]]
            for k in range(first, first + cols)
        ]

    def take(pieces, k):
        at = k % sub
        return pieces[k // sub][at:at + 1, :]

    def step(pieces, firsts, seconds, k, new_first, new_second, clear=None):
        out = []
        for g in range(height):
            base = pieces[g] if clear is None else jnp.where(clear, 0.0, pieces[g])
            value = base - firsts[g] * new_first - seconds[g] * new_second
            if g == k // sub:
                value = jnp.where(row == k % sub, new_first, value)
                value = jnp.where(row == k % sub + 1, new_second, value)
            out.append(value)
        return out

    now = columns(0)
    later = None
    for start in range(0, height * sub, cols):
        for j in range(0, cols, 2):
            k = start + j
            if j == cols // 2 and start + cols < height * sub:
                later = columns(start + cols)
            firsts, seconds = now[j], now[j + 1]
            a, b = take(firsts, k), take(seconds, k)
            c, d = take(firsts, k + 1), take(seconds, k + 1)
            scale = 1.0 / (a * d - b * c)
            a, b, c, d = d * scale, b * scale, c * scale, a * scale
            for i in range(j + 2, cols):
                up, down = take(now[i], k), take(now[i], k + 1)
                now[i] = step(now[i], firsts, seconds, k, a * up - b * down, d * down - c * up)
            if later is not None:
                for i in range(cols):
                    up, down = take(later[i], k), take(later[i], k + 1)
                    later[i] = step(
                        later[i], firsts, seconds, k, a * up - b * down, d * down - c * up
                    )
            for h, pieces in enumerate(tiles):
                up, down = take(pieces, k), take(pieces, k + 1)
                clear = None
                if h == 0:
                    at_up, at_down = lane == k, lane == k + 1
                    clear = at_up | at_down
                    up = jnp.where(at_up[:1], 1.0, jnp.where(at_down[:1], 0.0, up))
                    down = jnp.where(at_down[:1], 1.0, jnp.where(at_up[:1], 0.0, down))
                tiles[h] = step(
                    pieces, firsts, seconds, k, a * up - b * down, d * down - c * up, clear
                )
        now, later = later, None
    return tiles


def sweep_inverse(a_ref, beside=None, first=0, last=None):
    n = a_ref.shape[0]
    sub, wide = 8, 128
    lane = lax.broadcasted_iota(jnp.int32, (PANEL, n), 1)
    tile_lane = lax.broadcasted_iota(jnp.int32, (sub, wide), 1)
    tile_row = lax.broadcasted_iota(jnp.int32, (sub, wide), 0)

    def panel_step(step, carry):
        if beside is not None:
            beside(step)
        before = a_ref[:PANEL, :]
        tiles = [
            [before[g:g + sub, h:h + wide] for g in range(0, PANEL, sub)]
            for h in range(0, n, wide)
        ]
        tiles = pivot_panel(tiles, 8, tile_lane, tile_row)
        panel = jnp.concatenate([jnp.concatenate(pieces, axis=0) for pieces in tiles], axis=1)
        own = lane < PANEL
        update = jnp.where(own, -panel, panel)
        w_high, w_middle, w_low = split_three(before)
        z_high, z_middle, z_low = split_three(update)
        left = jnp.concatenate([w_low, w_middle, w_high, w_middle, w_high, w_high], axis=0)
        right = jnp.concatenate([z_high, z_middle, z_low, z_high, z_middle, z_high], axis=0)
        change = lax.dot_general(
            left, right, (((0,), (0,)), ((), ())), preferred_element_type=f32
        )
        others = jnp.where(own[:1], 0.0, a_ref[PANEL:, :]) - change[PANEL:, :]
        a_ref[:n - PANEL, :] = pltpu.roll(others, n - PANEL, 1)
        a_ref[n - PANEL:, :] = pltpu.roll(update, n - PANEL, 1)
        return carry

    lax.fori_loop(first, n // PANEL if last is None else last, panel_step, 0)


def sweep_kernel(
    edge, list_ref, x_hbm, orb_ref, nu_ref, a_out, b_out, c_out, scale_out, room, sems
):
    slots = list_ref.shape[1]
    here, size = lax.axis_index("orb"), lax.axis_size("orb")
    mine, count = lax.axis_index("aux"), lax.axis_size("aux")
    rank = nu_ref.shape[2]
    x_buf, parts, table, a_ref, e_ref, part = (
        room[name] for name in ("x", "parts", "table", "a", "e", "part")
    )
    work, even, odd = room["work"], room["even"], room["odd"]
    orb_rows, nu_rows = orb_ref.shape[0] * edge, nu_ref.shape[0] * edge
    first_base = mine * a_ref.shape[0]
    hop_send, hop_recv = sems["hop_send"], sems["hop_recv"]

    def load(slot):
        return pltpu.make_async_copy(x_hbm.at[slot], x_buf.at[slot], sems["x"].at[slot])

    def rows_of(ref, owner=mine):
        rows = ref.shape[0] // count
        return pl.ds(aligned(owner * rows, 8), rows)

    for slot in range(slots):
        load(slot).start()
    enter(("aux", "orb"))
    net = Net(sems["send"], sems["recv"])

    def part_rows(source, slot):
        return parts.at[pl.ds(aligned((source * slots + slot) * edge, edge), edge), :]

    def hop(way, distance, slot):
        rows = part_rows(here - way * distance, slot)
        lane = (1 - way) // 2
        return pltpu.make_async_remote_copy(
            src_ref=rows,
            dst_ref=rows,
            send_sem=hop_send.at[lane, distance, slot],
            recv_sem=hop_recv.at[lane, distance, slot],
            device_id={"orb": here + way},
            device_id_type=MESH,
        )

    def landed(way, distance, slot):
        rows = part_rows(here - way * distance, slot)
        lane = (1 - way) // 2
        return pltpu.make_async_remote_copy(
            src_ref=rows,
            dst_ref=rows,
            send_sem=hop_send.at[lane, distance - 1, slot],
            recv_sem=hop_recv.at[lane, distance - 1, slot],
            device_id={"orb": here - way},
            device_id_type=MESH,
        )

    def place(way):
        return (size - 1) * ((1 - way) // 2) + way * here

    def goes(way, distance):
        at = place(way)
        return (at + size - 1 - distance) // (size - 1) * ((2 * size - 3 - at) // (size - 1)) > 0

    def forward(distance, slot):
        for way in (1, -1):

            @pl.when(goes(way, distance))
            def _():
                landed(way, distance, slot).wait_recv()
                hop(way, distance, slot).start()

    def slot_step(slot, carry):
        load(slot).wait()
        nu_block = nu_ref[list_ref[2, slot]]
        orb_block = orb_ref[lax.rem(list_ref[1, slot], orb_ref.shape[0])]
        group = 4
        total = jnp.zeros((edge, rank), f32)
        for start in range(0, edge, group):
            x_high, x_low = split_two(x_buf[slot, :, start * edge:(start + group) * edge])
            stacked = jnp.concatenate([x_high, x_low], axis=0)
            product = jnp.concatenate(
                [nu_block * orb_block[j:j + 1, :] for j in range(start, start + group)], axis=0
            )
            high, low = split_two(product)
            main = jnp.dot(stacked, high, preferred_element_type=f32)
            rest = jnp.dot(x_high, low, preferred_element_type=f32)
            total += main[:edge] + (main[edge:] + rest)
        live = list_ref[3, slot].astype(f32)
        part_rows(here, slot)[...] = total * live
        for way in (1, -1):

            @pl.when(goes(way, 0))
            def _():
                hop(way, 0, slot).start()

        return carry

    early, late = slots // 4, slots - slots // 4
    lax.fori_loop(0, early, slot_step, 0)

    half = slots // 2
    row = lax.broadcasted_iota(jnp.int32, table.shape[1:], 0)
    for piece in range(2):
        own_at = jnp.zeros(table.shape[1:], f32)
        for slot in range(half):
            value = (list_ref[0, piece * half + slot] - first_base).astype(f32)
            own_at = jnp.where(row == slot, value, own_at)
        table[2 * here + piece] = own_at
    own_table = table.at[pl.ds(2 * here, 2)]
    table_copies = [
        net.copy(own_table, own_table, {"orb": (here + step) % size}) for step in range(1, size)
    ]
    orb_gram, orb_land, orb_sum = room["orb_gram"], room["orb_land"], room["orb_sum"]
    orb_gram[...] = gram_rows(orb_ref, even, odd)
    gram_copies = net.share("orb", orb_gram.at[rows_of(orb_gram), :], orb_land)
    room["s_nu"][...] = gram_rows(nu_ref, even, odd) / NU
    lax.fori_loop(early, late, slot_step, 0)
    arrive(gram_copies)
    orb_sum[rows_of(orb_sum), :] = total_of(orb_land)
    gram_copies = net.spread("aux", orb_sum, rank // count)
    lax.fori_loop(late, slots, slot_step, 0)

    if size > 2:

        def pass_near(slot, carry):
            forward(1, slot)
            return carry

        lax.fori_loop(0, slots, pass_near, 0)
    arrive(gram_copies)
    ridge = jnp.where(eye_mask(rank), ridge_weight, 0.0)
    work[...] = orb_sum[...] / (orb_rows * size) * room["s_nu"][...] + ridge
    panels = rank // PANEL
    together = panels == slots

    def beside(step):
        if size > 3:
            forward(2, step)

    sweep_inverse(work, beside if together else None)
    for at, piece in enumerate(split_three(-work[...])):
        room["inverse"][at] = piece
    for distance in range(3 if together else 2, size - 1):

        def pass_on(slot, carry, distance=distance):
            forward(distance, slot)
            return carry

        lax.fori_loop(0, slots, pass_on, 0)
    arrive(table_copies)

    def add_rows(source, piece, clear):
        start = piece * half
        rows = parts[pl.ds(aligned((source * slots + start) * edge, edge), half * edge), :]
        inverse = tuple(room["inverse"][at] for at in range(3))
        room["q"][...] = dot_exact(split_three(rows), inverse)
        places = table[2 * source + piece]

        def block_step(block, carry):
            name = jnp.full((1, rank), block, jnp.int32).astype(f32)
            total = jnp.zeros((edge, rank), f32) if clear else a_ref[block]
            for slot in range(half):
                weight = jnp.where(places[slot:slot + 1, :] == name, 1.0, 0.0)
                total += room["q"][slot * edge:(slot + 1) * edge, :] * weight
            a_ref[block] = total
            return carry

        lax.fori_loop(0, a_ref.shape[0], block_step, 0)

    add_rows(here, 0, True)
    add_rows(here, 1, False)

    def source_step(at, carry):
        distance, way = at // 2 + 1, 1 - at % 2 * 2
        source = here - way * distance

        @pl.when((source + size) // size * ((2 * size - 1 - source) // size) > 0)
        def _():
            def half_step(piece, carry):
                @pl.when(place(way) == size - 1)
                def _():
                    for slot in range(half):
                        landed(way, distance, piece * half + slot).wait_recv()

                add_rows(source, piece, False)
                return carry

            lax.fori_loop(0, 2, half_step, 0)

        return carry

    lax.fori_loop(0, 2 * (size - 1), source_step, 0)
    save_a = pltpu.make_async_copy(a_ref, a_out, sems["save"].at[0])
    save_a.start()

    gram_a, gram_land = room["gram_a"], room["gram_land"]
    room["gram"][...] = gram_rows(a_ref, even, odd)
    gram_copies = net.scatter("aux", room["gram"], gram_land)

    def second_step(slot, carry):
        nu_block = nu_ref[list_ref[2, slot]]
        a_high, a_low = split_two(a_ref[lax.rem(list_ref[0, slot], a_ref.shape[0])])
        weights = jnp.concatenate([a_high, a_high, a_low, a_low], axis=0)
        group = 8
        for start in range(0, edge, group):
            x_high, x_low = split_two(x_buf[slot, :, start * edge:(start + group) * edge])
            turned = jnp.concatenate([x_high, x_low], axis=0).T
            e = jnp.dot(
                jnp.concatenate([turned, turned], axis=1), weights, preferred_element_type=f32
            )
            e_ref[slot, start * edge:(start + group) * edge, :] = e
            part[slot, start:start + group, :] = jnp.sum(
                e.reshape(group, edge, rank) * nu_block[None], axis=1
            )
        return carry

    def gather_blocks(dimension, out_ref):
        blocks = out_ref.shape[0] // edge
        places = [lax.rem(list_ref[dimension, slot], blocks) for slot in range(slots)]
        lives = [list_ref[3, slot].astype(f32) for slot in range(slots)]

        def block_step(block, carry):
            total = jnp.zeros((edge, rank), f32)
            for slot in range(slots):
                weight = (places[slot] == block).astype(f32) * lives[slot]
                total += part[slot] * weight
            out_ref[pl.ds(aligned(block * edge, edge), edge), :] = total
            return carry

        lax.fori_loop(0, blocks, block_step, 0)

    lax.fori_loop(0, half, second_step, 0)
    arrive(gram_copies)
    gram_a[rows_of(gram_a), :] = total_of(gram_land)
    gram_copies = net.spread("aux", gram_a, rank // count)
    lax.fori_loop(half, slots, second_step, 0)
    gather_blocks(1, room["terms"])
    terms_copies = net.scatter("aux", room["terms"], room["terms_land"])

    arrive(gram_copies)
    unit_a, scale_a = unit_gram(gram_a[...], P_SIZE)
    work[...] = unit_a * room["s_nu"][...] + ridge
    sweep_inverse(work)
    inverse = split_three(-work[...])
    arrive(terms_copies)
    b_full, b_blocks = room["b"], room["b_blocks"]
    b_full[rows_of(b_full), :] = dot_exact(
        split_three(total_of(room["terms_land"]) / scale_a), inverse
    )
    even[...] = jnp.zeros_like(even)
    odd[...] = jnp.zeros_like(odd)

    def b_landed(owner):
        gram_add(b_full[rows_of(b_full, owner), :], even, odd)

    net.spread_pairs("aux", b_full, orb_rows // count, b_landed)
    gram_b = room["gram_b"]
    cross = odd[...]
    gram_b[...] = even[...] + (cross + cross.T)
    z_copies = net.share("orb", gram_b.at[rows_of(gram_b), :], room["z_land"])
    save_b = pltpu.make_async_copy(b_full, b_out, sems["save"].at[1])
    save_b.start()
    b_blocks[...] = b_full[...].reshape(b_blocks.shape)

    def third_step(slot, carry):
        b_block = b_blocks[lax.rem(list_ref[1, slot], b_blocks.shape[0])]
        total = jnp.zeros((edge, rank), f32)
        for j in range(edge):
            total += e_ref[slot, j * edge:(j + 1) * edge, :] * b_block[j:j + 1, :]
        part[slot] = total
        return carry

    gram_sum = room["gram_sum"]
    thirds, thirds_land, third_sums = room["thirds"], room["thirds_land"], room["third_sums"]
    lax.fori_loop(0, half, third_step, 0)
    arrive(z_copies)
    gram_sum[rows_of(gram_sum), :] = total_of(room["z_land"])
    gram_copies = net.spread("aux", gram_sum, rank // count)
    lax.fori_loop(half, slots, third_step, 0)
    gather_blocks(2, thirds)
    third_copies = net.scatter("aux", thirds, thirds_land)

    arrive(gram_copies)
    unit_b, scale_b = unit_gram(gram_sum[...], orb_rows * size)
    work[...] = unit_b * unit_gram(gram_a[...], P_SIZE)[0] + ridge
    sweep_inverse(work, None, 0, panels // 2)
    arrive(third_copies)
    thirds_land[mine] = total_of(thirds_land)
    third_copies = net.share("orb", thirds_land.at[mine], room["thirds_z"])
    sweep_inverse(work, None, panels // 2, panels)
    inverse = split_three(-work[...])
    arrive(third_copies)
    third_sums[rows_of(third_sums), :] = total_of(room["thirds_z"])
    net.spread_pairs("aux", third_sums, nu_rows // count)
    c_new = dot_exact(split_three(third_sums[...] / scale_a / scale_b), inverse)
    scale_c = jnp.sqrt(jnp.sum(c_new * c_new, axis=0, keepdims=True) / nu_rows + epsilon)
    c_out[...] = c_new
    scale_out[0:1, :] = scale_a
    scale_out[1:2, :] = scale_b
    scale_out[2:3, :] = scale_c

    def last(slot, carry):
        for way in (1, -1):
            for distance in range(size - 1):

                @pl.when(goes(way, distance))
                def _():
                    hop(way, distance, slot).wait_send()

        return carry

    lax.fori_loop(0, slots, last, 0)
    save_a.wait()
    save_b.wait()
    net.finish()


def scale_kernel(a_hbm, b_hbm, c_hbm, scale_ref, a_out, b_out, c_out, a, b, c, load_sem, save_sem):
    pieces = []
    for at, (source, target, buffer) in enumerate(
        ((a_hbm, a_out, a), (b_hbm, b_out, b), (c_hbm, c_out, c))
    ):
        step = min(512, buffer.shape[0])
        for start in range(0, buffer.shape[0], step):
            number = len(pieces)
            rows = pl.ds(start, step)
            pieces.append(
                (
                    at,
                    buffer,
                    rows,
                    pltpu.make_async_copy(
                        source.at[rows, :], buffer.at[rows, :], load_sem.at[number]
                    ),
                    pltpu.make_async_copy(
                        buffer.at[rows, :], target.at[rows, :], save_sem.at[number]
                    ),
                )
            )
    for piece in pieces:
        piece[3].start()
    for at, buffer, rows, load, save in pieces:
        load.wait()
        buffer[rows, :] = buffer[rows, :] / scale_ref[at:at + 1, :]
        save.start()
    for piece in pieces:
        piece[4].wait()


def per_device(tiles, tile_list, orb_factor, nu_factor):
    slots, edge, tile_width = tiles.shape
    rank = nu_factor.shape[1]
    aux_size, orb_size = lax.axis_size("aux"), lax.axis_size("orb")
    first_rows = P_SIZE // aux_size
    orb_rows, nu_rows = orb_factor.shape[0], nu_factor.shape[0]
    square = (rank, rank)
    shapes = {
        "x": (slots, edge, tile_width),
        "parts": (orb_size * slots * edge, rank),
        "table": (orb_size * 2, 8, rank),
        "a": (first_rows // edge, edge, rank),
        "e": (slots, tile_width, rank),
        "part": (slots, edge, rank),
        "q": (slots // 2 * edge, rank),
        "orb_land": (orb_size, rank // aux_size, rank),
        "gram_land": (aux_size, rank // aux_size, rank),
        "terms": (orb_rows, rank),
        "terms_land": (aux_size, orb_rows // aux_size, rank),
        "b": (orb_rows, rank),
        "b_blocks": (orb_rows // edge, edge, rank),
        "z_land": (orb_size, rank // aux_size, rank),
        "thirds": (nu_rows, rank),
        "thirds_land": (aux_size, nu_rows // aux_size, rank),
        "thirds_z": (orb_size, nu_rows // aux_size, rank),
        "third_sums": (nu_rows, rank),
    }
    for name in ("work", "even", "odd", "orb_gram", "orb_sum", "s_nu", "gram", "gram_a", "gram_b", "gram_sum"):
        shapes[name] = square
    net_count = 8 * (aux_size - 1) + 4 * (orb_size - 1)
    dma = pltpu.SemaphoreType.DMA
    semaphores = {
        "x": dma((slots,)),
        "send": dma((net_count,)),
        "recv": dma((net_count,)),
        "hop_send": dma((2, orb_size - 1, slots)),
        "hop_recv": dma((2, orb_size - 1, slots)),
        "save": dma((2,)),
    }
    room = {name: pltpu.VMEM(shape, f32) for name, shape in shapes.items()}
    room["inverse"] = pltpu.VMEM((3,) + square, bf16)
    vmem = pl.BlockSpec(memory_space=pltpu.VMEM)
    hbm = pl.BlockSpec(memory_space=pltpu.HBM)

    def kernel(list_ref, x_hbm, orb_ref, nu_ref, a_out, b_out, c_out, scale_out, *scratch):
        names = list(room)
        sweep_kernel(
            edge, list_ref, x_hbm, orb_ref, nu_ref, a_out, b_out, c_out, scale_out,
            dict(zip(names, scratch)), dict(zip(semaphores, scratch[len(names):]))
        )

    a_new, b_new, c_new, scales = pl.pallas_call(
        kernel,
        out_shape=(
            jax.ShapeDtypeStruct((first_rows // edge, edge, rank), f32),
            jax.ShapeDtypeStruct((orb_rows, rank), f32),
            jax.ShapeDtypeStruct((nu_rows, rank), f32),
            jax.ShapeDtypeStruct((8, rank), f32),
        ),
        in_specs=[pl.BlockSpec(memory_space=pltpu.SMEM), hbm, vmem, vmem],
        out_specs=(hbm, hbm, vmem, vmem),
        scratch_shapes=list(room.values()) + list(semaphores.values()),
        compiler_params=pltpu.CompilerParams(
            collective_id=5, has_side_effects=True, vmem_limit_bytes=62 << 20
        ),
        name="sweep",
    )(tile_list, tiles, orb_factor.reshape(-1, edge, rank), nu_factor.reshape(-1, edge, rank))
    rows = (first_rows, orb_rows, nu_rows)
    count = sum(-(-size // 512) for size in rows)
    return pl.pallas_call(
        scale_kernel,
        out_shape=tuple(jax.ShapeDtypeStruct((size, rank), f32) for size in rows),
        in_specs=[hbm, hbm, hbm, vmem],
        out_specs=(hbm, hbm, hbm),
        scratch_shapes=[pltpu.VMEM((size, rank), f32) for size in rows]
        + [dma((count,)), dma((count,))],
        compiler_params=pltpu.CompilerParams(vmem_limit_bytes=60 << 20),
        name="scale",
    )(a_new.reshape(first_rows, rank), b_new, c_new, scales)


def solution(mesh):
    return jax.shard_map(
        per_device,
        mesh=mesh,
        in_specs=(P(("aux", "orb"), None, None), P(None, ("aux", "orb")), P("orb", None), P()),
        out_specs=(P("aux", None), P("orb", None), P()),
        check_vma=False,
    )
```

time: 134 us -> 115 us (0.86)
  Pallas kernels: 128 us -> 113 us
  local copies, waits for them, and re-layouts: 3.03 us -> 0 us
  other arithmetic: 1.46 us -> 0 us
    pallas_call x3 -> x2, Pallas kernels: 128 us -> 113 us  [the longest x1 109 us: per_device(): pl.pallas_call(kernel, out_shape=(jax.ShapeDtypeStruct((first_rows // edg...]
    unnamed x8 -> x0, local copies, waits for them, and re-layouts: 2.33 us -> none
    div x1 -> x0, other arithmetic: 1.46 us -> none  [per_device(): return (a_new / scale[:1], orb_updated, nu_updated)]
where the time goes in v4:
time: 115 us; the launch traced here: 114 us
  Pallas kernels  113 us (98%)
    pallas_call x1, Pallas kernels, per_device(): pl.pallas_call(kernel, out_shape=(jax.ShapeDtypeStruct((first_rows // edg...  109 us
    pallas_call x1, Pallas kernels, per_device(): pl.pallas_call(scale_kernel, out_shape=tuple((jax.ShapeDtypeStruct((size,...  3.73 us

profile of v4, /device:TPU:0, one launch (start us, length us, event | category | flops | bytes accessed | tf_op | source)
XLA Modules:
  0.0 114.0 jit_solution(12775255718819349451)
XLA Ops:
  0.6 109.5 %sweep.1 = (f32[32,64,256]{2,1,0:T(8,128)}, f32[1024,256]{1,0:T(8,128)}, f32[512,256]{1,0:T(8,128)}, f32[8,256]{1,0:T(8,128)}) custom-call(s32[4,8]{1,0:T(4,128)} %list_ref.1, f32[8,64,4096]{2,1,0:T(8,128)} %x_hbm.1, f32[16,64,256]{2,1,0:T(8,128)} %bitcast.4, f32[8,64,256]{2,1,0:T(8,128)} %bitcast.5), custom_call_target="tpu_custom_call" | custom-call | tf_op jit(solution)/shard_map/sweep/pallas_call | solution.py:679
  110.1 3.7 %scale.1 = (f32[2048,256]{1,0:T(8,128)}, f32[1024,256]{1,0:T(8,128)}, f32[512,256]{1,0:T(8,128)}) custom-call(f32[2048,256]{1,0:T(8,128)} %bitcast.3, f32[1024,256]{1,0:T(8,128)} %get-tuple-element.8.b_hbm, f32[512,256]{1,0:T(8,128)} %get-tuple-element.9.c_hbm, f32[8,256]{1,0:T(8,128)} %get-tuple-element.10.scale_ref), custom_call_target="tpu_custom_call" | custom-call | tf_op jit(solution)/shard_map/scale/pallas_call | solution.py:697

commit v5 on v4

--- a/solution.py
+++ b/solution.py
@@ -52,11 +52,8 @@
 
 def gram_add(x, even_ref, odd_ref):
     high, middle, low = split_three(x)
-    pair = jnp.concatenate([high, middle], axis=0)
-    even_ref[...] += dot_t(pair, pair)
-    odd_ref[...] += dot_t(
-        jnp.concatenate([high, high], axis=0), jnp.concatenate([middle, low], axis=0)
-    )
+    even_ref[...] += dot_t(high, high) + dot_t(middle, middle)
+    odd_ref[...] += dot_t(high, middle) + dot_t(high, low)
 
 
 def gram_rows(x_ref, even_ref, odd_ref):
@@ -91,7 +88,7 @@
     def __init__(self, send, recv):
         self.send, self.recv, self.copies = send, recv, []
 
-    def copy(self, src, dst, to):
+    def plan(self, src, dst, to):
         at = len(self.copies)
         copy = pltpu.make_async_remote_copy(
             src_ref=src,
@@ -101,8 +98,12 @@
             device_id=to,
             device_id_type=MESH,
         )
+        self.copies.append(copy)
+        return copy
+
+    def copy(self, src, dst, to):
+        copy = self.plan(src, dst, to)
         copy.start()
-        self.copies.append(copy)
         return copy
 
     def scatter(self, axis, src, land):
@@ -128,36 +129,82 @@
         own = full.at[pl.ds(aligned(here * rows, 8), rows), :]
         return [self.copy(own, own, {axis: (here + step) % size}) for step in range(1, size)]
 
-    def spread_pairs(self, axis, full, rows, landed=None):
+    def finish(self):
+        for copy in self.copies:
+            copy.wait_send()
+
+
+class PairSpread:
+    def __init__(self, net, axis, block):
         size, here = lax.axis_size(axis), lax.axis_index(axis)
         chips, chip, core = size // 2, here // 2, here % 2
         other = here + 1 - 2 * core
-
-        def block(owner):
-            return full.at[pl.ds(aligned(owner * rows, 8), rows), :]
-
+        self.own = here
+        self.near_from = [chip * 2 + 1 - core]
+        self.far_from, self.far, self.relays = [], [], []
         own = block(here)
-        far = [
-            self.copy(own, own, {axis: (chip + step) % chips * 2 + core})
-            for step in range(1, chips)
-        ]
-        near = [self.copy(own, own, {axis: other})]
-        if landed is not None:
-            landed(here)
-        for step, copy in enumerate(far, 1):
+        self.near = [net.plan(own, own, {axis: other})]
+        for step in range(1, chips):
+            target = (chip + step) % chips * 2 + core
+            self.far.append(net.plan(own, own, {axis: target}))
             source = (chip + chips - step) % chips * 2
+            self.far_from.append(source + core)
+            self.near_from.append(source + 1 - core)
+            passed = block(source + core)
+            self.near.append(net.plan(passed, passed, {axis: other}))
+
+    def start(self):
+        for copy in self.far:
+            copy.start()
+        self.near[0].start()
+
+    def relay(self, landed=None):
+        for copy, near, owner in zip(self.far, self.near[1:], self.far_from):
             copy.wait_recv()
-            near.append(self.copy(block(source + core), block(source + core), {axis: other}))
+            near.start()
             if landed is not None:
-                landed(source + core)
-        for step, copy in enumerate(near):
+                landed(owner)
+
+    def collect(self, landed=None):
+        for copy, owner in zip(self.near, self.near_from):
             copy.wait_recv()
             if landed is not None:
-                landed((chip + chips - step) % chips * 2 + 1 - core)
-
-    def finish(self):
-        for copy in self.copies:
-            copy.wait_send()
+                landed(owner)
+
+
+class PairScatter:
+    def __init__(self, net, axis, block, pair, stage, land):
+        size, here = lax.axis_size(axis), lax.axis_index(axis)
+        chips, chip, core = size // 2, here // 2, here % 2
+        other = here + 1 - 2 * core
+        self.chip, self.land, self.pair, self.stage = chip, land, pair, stage
+        self.first, self.second, self.targets = [], [], []
+        for step in range(1, chips + 1):
+            target = (chip + step) % chips
+            self.targets.append((target, block(target * 2 + core)))
+            away = block(target * 2 + 1 - core)
+            self.first.append(net.plan(away, pair.at[target], {axis: other}))
+            if step < chips:
+                self.second.append(
+                    net.plan(stage.at[target], land.at[chip], {axis: target * 2 + core})
+                )
+
+    def start(self):
+        for copy in self.first:
+            copy.start()
+
+    def relay(self):
+        for copy, send, (target, own) in zip(self.first, self.second, self.targets):
+            copy.wait_recv()
+            self.stage[target] = own[...] + self.pair[target]
+            send.start()
+        self.first[-1].wait_recv()
+        target, own = self.targets[-1]
+        self.land[self.chip] = own[...] + self.pair[target]
+
+    def total(self):
+        arrive(self.second)
+        return total_of(self.land)
 
 
 def arrive(copies):
@@ -492,16 +539,16 @@
             )
         return carry
 
-    def gather_blocks(dimension, out_ref):
+    def gather_blocks(dimension, out_ref, columns=slice(None)):
         blocks = out_ref.shape[0] // edge
         places = [lax.rem(list_ref[dimension, slot], blocks) for slot in range(slots)]
         lives = [list_ref[3, slot].astype(f32) for slot in range(slots)]
 
         def block_step(block, carry):
-            total = jnp.zeros((edge, rank), f32)
+            total = jnp.zeros((edge, out_ref.shape[1]), f32)
             for slot in range(slots):
                 weight = (places[slot] == block).astype(f32) * lives[slot]
-                total += part[slot] * weight
+                total += part[slot, :, columns] * weight
             out_ref[pl.ds(aligned(block * edge, edge), edge), :] = total
             return carry
 
@@ -513,17 +560,27 @@
     gram_copies = net.spread("aux", gram_a, rank // count)
     lax.fori_loop(half, slots, second_step, 0)
     gather_blocks(1, room["terms"])
-    terms_copies = net.scatter("aux", room["terms"], room["terms_land"])
+    terms = room["terms"]
+    terms_sum = PairScatter(
+        net, "aux", lambda owner: terms.at[rows_of(terms, owner), :],
+        room["terms_pair"], room["terms_stage"], room["terms_land"]
+    )
+    terms_sum.start()
 
     arrive(gram_copies)
     unit_a, scale_a = unit_gram(gram_a[...], P_SIZE)
     work[...] = unit_a * room["s_nu"][...] + ridge
-    sweep_inverse(work)
+
+    def beside_second(step):
+        @pl.when(step == 1)
+        def _():
+            terms_sum.relay()
+
+    sweep_inverse(work, beside_second)
     inverse = split_three(-work[...])
-    arrive(terms_copies)
     b_full, b_blocks = room["b"], room["b_blocks"]
     b_full[rows_of(b_full), :] = dot_exact(
-        split_three(total_of(room["terms_land"]) / scale_a), inverse
+        split_three(terms_sum.total() / scale_a), inverse
     )
     even[...] = jnp.zeros_like(even)
     odd[...] = jnp.zeros_like(odd)
@@ -531,7 +588,11 @@
     def b_landed(owner):
         gram_add(b_full[rows_of(b_full, owner), :], even, odd)
 
-    net.spread_pairs("aux", b_full, orb_rows // count, b_landed)
+    b_spread = PairSpread(net, "aux", lambda owner: b_full.at[rows_of(b_full, owner), :])
+    b_spread.start()
+    b_landed(mine)
+    b_spread.relay(b_landed)
+    b_spread.collect(b_landed)
     gram_b = room["gram_b"]
     cross = odd[...]
     gram_b[...] = even[...] + (cross + cross.T)
@@ -540,37 +601,90 @@
     save_b.start()
     b_blocks[...] = b_full[...].reshape(b_blocks.shape)
 
-    def third_step(slot, carry):
-        b_block = b_blocks[lax.rem(list_ref[1, slot], b_blocks.shape[0])]
-        total = jnp.zeros((edge, rank), f32)
-        for j in range(edge):
-            total += e_ref[slot, j * edge:(j + 1) * edge, :] * b_block[j:j + 1, :]
-        part[slot] = total
-        return carry
-
     gram_sum = room["gram_sum"]
-    thirds, thirds_land, third_sums = room["thirds"], room["thirds_land"], room["third_sums"]
-    lax.fori_loop(0, half, third_step, 0)
+    thirds, thirds_land, thirds_z, third_sums = (
+        room[name] for name in ("thirds", "thirds_land", "thirds_z", "third_sums")
+    )
+    wide = rank // 2
+
+    def third_half(side):
+        columns = slice(side * wide, (side + 1) * wide)
+
+        def third_step(slot, carry):
+            b_block = b_blocks[lax.rem(list_ref[1, slot], b_blocks.shape[0])][:, columns]
+            total = jnp.zeros((edge, wide), f32)
+            for j in range(edge):
+                total += e_ref[slot, j * edge:(j + 1) * edge, columns] * b_block[j:j + 1, :]
+            part[slot, :, columns] = total
+            return carry
+
+        lax.fori_loop(0, slots, third_step, 0)
+        gather_blocks(2, thirds.at[side], columns)
+
+    def third_spread(side):
+        full = third_sums.at[side]
+        rows = nu_rows // count
+        return PairSpread(
+            net, "aux", lambda owner: full.at[pl.ds(aligned(owner * rows, 8), rows), :]
+        )
+
+    third_half(0)
+    third_copies = [net.scatter("aux", thirds.at[0], thirds_land.at[0])]
+    third_half(1)
     arrive(z_copies)
     gram_sum[rows_of(gram_sum), :] = total_of(room["z_land"])
-    gram_copies = net.spread("aux", gram_sum, rank // count)
-    lax.fori_loop(half, slots, third_step, 0)
-    gather_blocks(2, thirds)
-    third_copies = net.scatter("aux", thirds, thirds_land)
-
-    arrive(gram_copies)
+    gram_spread = PairSpread(net, "aux", lambda owner: gram_sum.at[rows_of(gram_sum, owner), :])
+    gram_spread.start()
+    third_copies.append(net.scatter("aux", thirds.at[1], thirds_land.at[1]))
+    shares, spreads = [], []
+    for side in range(2):
+        own = thirds_land.at[side, mine]
+        shares.append(
+            [
+                net.plan(own, thirds_z.at[side, here], {"orb": (here + step) % size})
+                for step in range(1, size)
+            ]
+        )
+        spreads.append(third_spread(side))
+
+    def third_landed(side):
+        arrive(third_copies[side])
+        total = total_of(thirds_land.at[side])
+        thirds_land[side, mine] = total
+        thirds_z[side, here] = total
+        for copy in shares[side]:
+            copy.start()
+
+    def third_summed(side):
+        arrive(shares[side])
+        third_sums[side, pl.ds(aligned(mine * (nu_rows // count), 8), nu_rows // count), :] = (
+            total_of(thirds_z.at[side])
+        )
+        spreads[side].start()
+
+    gram_spread.relay()
+    gram_spread.collect()
     unit_b, scale_b = unit_gram(gram_sum[...], orb_rows * size)
     work[...] = unit_b * unit_gram(gram_a[...], P_SIZE)[0] + ridge
-    sweep_inverse(work, None, 0, panels // 2)
-    arrive(third_copies)
-    thirds_land[mine] = total_of(thirds_land)
-    third_copies = net.share("orb", thirds_land.at[mine], room["thirds_z"])
-    sweep_inverse(work, None, panels // 2, panels)
+
+    def beside_third(step):
+        for when, act, side in (
+            (1, third_landed, 0), (3, third_landed, 1), (panels - 1, third_summed, 0)
+        ):
+
+            @pl.when(step == when)
+            def _():
+                act(side)
+
+    sweep_inverse(work, beside_third)
     inverse = split_three(-work[...])
-    arrive(third_copies)
-    third_sums[rows_of(third_sums), :] = total_of(room["thirds_z"])
-    net.spread_pairs("aux", third_sums, nu_rows // count)
-    c_new = dot_exact(split_three(third_sums[...] / scale_a / scale_b), inverse)
+    spreads[0].relay()
+    third_summed(1)
+    spreads[0].collect()
+    spreads[1].relay()
+    spreads[1].collect()
+    third_all = jnp.concatenate([third_sums[0], third_sums[1]], axis=1)
+    c_new = dot_exact(split_three(third_all / scale_a / scale_b), inverse)
     scale_c = jnp.sqrt(jnp.sum(c_new * c_new, axis=0, keepdims=True) / nu_rows + epsilon)
     c_out[...] = c_new
     scale_out[0:1, :] = scale_a
@@ -643,18 +757,20 @@
         "orb_land": (orb_size, rank // aux_size, rank),
         "gram_land": (aux_size, rank // aux_size, rank),
         "terms": (orb_rows, rank),
-        "terms_land": (aux_size, orb_rows // aux_size, rank),
+        "terms_pair": (aux_size // 2, orb_rows // aux_size, rank),
+        "terms_stage": (aux_size // 2, orb_rows // aux_size, rank),
+        "terms_land": (aux_size // 2, orb_rows // aux_size, rank),
         "b": (orb_rows, rank),
         "b_blocks": (orb_rows // edge, edge, rank),
         "z_land": (orb_size, rank // aux_size, rank),
-        "thirds": (nu_rows, rank),
-        "thirds_land": (aux_size, nu_rows // aux_size, rank),
-        "thirds_z": (orb_size, nu_rows // aux_size, rank),
-        "third_sums": (nu_rows, rank),
+        "thirds": (2, nu_rows, rank // 2),
+        "thirds_land": (2, aux_size, nu_rows // aux_size, rank // 2),
+        "thirds_z": (2, orb_size, nu_rows // aux_size, rank // 2),
+        "third_sums": (2, nu_rows, rank // 2),
     }
     for name in ("work", "even", "odd", "orb_gram", "orb_sum", "s_nu", "gram", "gram_a", "gram_b", "gram_sum"):
         shapes[name] = square
-    net_count = 8 * (aux_size - 1) + 4 * (orb_size - 1)
+    net_count = 10 * (aux_size - 1) + 5 * (orb_size - 1)
     dma = pltpu.SemaphoreType.DMA
     semaphores = {
         "x": dma((slots,)),

time: 115 us -> 113 us (0.983)
    pallas_call x1, Pallas kernels: 109 us -> 108 us  [per_device(): pl.pallas_call(kernel, out_shape=(jax.ShapeDtypeStruct((first_rows // edg...]
where the time goes in v5:
time: 113 us; the launch traced here: 112 us
  Pallas kernels  112 us (99%)
    pallas_call x1, Pallas kernels, per_device(): pl.pallas_call(kernel, out_shape=(jax.ShapeDtypeStruct((first_rows // edg...  108 us
    pallas_call x1, Pallas kernels, per_device(): pl.pallas_call(scale_kernel, out_shape=tuple((jax.ShapeDtypeStruct((size,...  3.73 us

profile of v5, /device:TPU:0, one launch (start us, length us, event | category | flops | bytes accessed | tf_op | source)
XLA Modules:
  0.0 112.4 jit_solution(2785693336511777333)
XLA Ops:
  0.6 107.8 %sweep.1 = (f32[32,64,256]{2,1,0:T(8,128)}, f32[1024,256]{1,0:T(8,128)}, f32[512,256]{1,0:T(8,128)}, f32[8,256]{1,0:T(8,128)}) custom-call(s32[4,8]{1,0:T(4,128)} %list_ref.1, f32[8,64,4096]{2,1,0:T(8,128)} %x_hbm.1, f32[16,64,256]{2,1,0:T(8,128)} %bitcast.4, f32[8,64,256]{2,1,0:T(8,128)} %bitcast.5), custom_call_target="tpu_custom_call" | custom-call | tf_op jit(solution)/shard_map/sweep/pallas_call | solution.py:795
  108.5 3.7 %scale.1 = (f32[2048,256]{1,0:T(8,128)}, f32[1024,256]{1,0:T(8,128)}, f32[512,256]{1,0:T(8,128)}) custom-call(f32[2048,256]{1,0:T(8,128)} %bitcast.3, f32[1024,256]{1,0:T(8,128)} %get-tuple-element.8.b_hbm, f32[512,256]{1,0:T(8,128)} %get-tuple-element.9.c_hbm, f32[8,256]{1,0:T(8,128)} %get-tuple-element.10.scale_ref), custom_call_target="tpu_custom_call" | custom-call | tf_op jit(solution)/shard_map/scale/pallas_call | solution.py:813

commit v6 on v5

--- a/solution.py
+++ b/solution.py
@@ -59,7 +59,7 @@
 def gram_rows(x_ref, even_ref, odd_ref):
     even_ref[...] = jnp.zeros_like(even_ref)
     odd_ref[...] = jnp.zeros_like(odd_ref)
-    group = min(4, x_ref.shape[0])
+    group = min(8, x_ref.shape[0])
 
     def step(at, carry):
         rows = x_ref[pl.ds(at * group, group)]
@@ -260,7 +260,7 @@
     for start in range(0, height * sub, cols):
         for j in range(0, cols, 2):
             k = start + j
-            if j == cols // 2 and start + cols < height * sub:
+            if j == cols - 2 and start + cols < height * sub:
                 later = columns(start + cols)
             firsts, seconds = now[j], now[j + 1]
             a, b = take(firsts, k), take(seconds, k)
@@ -663,13 +663,14 @@
         spreads[side].start()
 
     gram_spread.relay()
+    third_landed(0)
     gram_spread.collect()
     unit_b, scale_b = unit_gram(gram_sum[...], orb_rows * size)
     work[...] = unit_b * unit_gram(gram_a[...], P_SIZE)[0] + ridge
 
     def beside_third(step):
         for when, act, side in (
-            (1, third_landed, 0), (3, third_landed, 1), (panels - 1, third_summed, 0)
+            (2, third_landed, 1), (panels - 3, third_summed, 0)
         ):
 
             @pl.when(step == when)
@@ -678,11 +679,11 @@
 
     sweep_inverse(work, beside_third)
     inverse = split_three(-work[...])
-    spreads[0].relay()
     third_summed(1)
-    spreads[0].collect()
-    spreads[1].relay()
-    spreads[1].collect()
+    for spread in spreads:
+        spread.relay()
+    for spread in spreads:
+        spread.collect()
     third_all = jnp.concatenate([third_sums[0], third_sums[1]], axis=1)
     c_new = dot_exact(split_three(third_all / scale_a / scale_b), inverse)
     scale_c = jnp.sqrt(jnp.sum(c_new * c_new, axis=0, keepdims=True) / nu_rows + epsilon)

time: 113 us -> 109 us (0.965)
  Pallas kernels: 112 us -> 108 us
    pallas_call x1, Pallas kernels: 108 us -> 104 us  [per_device(): pl.pallas_call(kernel, out_shape=(jax.ShapeDtypeStruct((first_rows // edg...]
where the time goes in v6:
time: 109 us; the launch traced here: 108 us
  Pallas kernels  108 us (99%)
    pallas_call x1, Pallas kernels, per_device(): pl.pallas_call(kernel, out_shape=(jax.ShapeDtypeStruct((first_rows // edg...  104 us
    pallas_call x1, Pallas kernels, per_device(): pl.pallas_call(scale_kernel, out_shape=tuple((jax.ShapeDtypeStruct((size,...  3.73 us

profile of v6, /device:TPU:0, one launch (start us, length us, event | category | flops | bytes accessed | tf_op | source)
XLA Modules:
  0.0 108.3 jit_solution(15017584381076832661)
XLA Ops:
  0.6 103.8 %sweep.1 = (f32[32,64,256]{2,1,0:T(8,128)}, f32[1024,256]{1,0:T(8,128)}, f32[512,256]{1,0:T(8,128)}, f32[8,256]{1,0:T(8,128)}) custom-call(s32[4,8]{1,0:T(4,128)} %list_ref.1, f32[8,64,4096]{2,1,0:T(8,128)} %x_hbm.1, f32[16,64,256]{2,1,0:T(8,128)} %bitcast.4, f32[8,64,256]{2,1,0:T(8,128)} %bitcast.5), custom_call_target="tpu_custom_call" | custom-call | tf_op jit(solution)/shard_map/sweep/pallas_call | solution.py:796
  104.4 3.7 %scale.1 = (f32[2048,256]{1,0:T(8,128)}, f32[1024,256]{1,0:T(8,128)}, f32[512,256]{1,0:T(8,128)}) custom-call(f32[2048,256]{1,0:T(8,128)} %bitcast.3, f32[1024,256]{1,0:T(8,128)} %get-tuple-element.8.b_hbm, f32[512,256]{1,0:T(8,128)} %get-tuple-element.9.c_hbm, f32[8,256]{1,0:T(8,128)} %get-tuple-element.10.scale_ref), custom_call_target="tpu_custom_call" | custom-call | tf_op jit(solution)/shard_map/scale/pallas_call | solution.py:814

commit v7 on v6

--- a/solution.py
+++ b/solution.py
@@ -326,8 +326,9 @@
 
 
 def sweep_kernel(
-    edge, list_ref, x_hbm, orb_ref, nu_ref, a_out, b_out, c_out, scale_out, room, sems
+    edge, list_ref, x_hbm, orb_hbm, nu_hbm, a_out, b_out, c_out, scale_out, room, sems
 ):
+    orb_ref, nu_ref = room["orb"], room["nu"]
     slots = list_ref.shape[1]
     here, size = lax.axis_index("orb"), lax.axis_size("orb")
     mine, count = lax.axis_index("aux"), lax.axis_size("aux")
@@ -347,9 +348,20 @@
         rows = ref.shape[0] // count
         return pl.ds(aligned(owner * rows, 8), rows)
 
-    for slot in range(slots):
+    factor_loads = (
+        pltpu.make_async_copy(nu_hbm, nu_ref, sems["factors"].at[0]),
+        pltpu.make_async_copy(orb_hbm, orb_ref, sems["factors"].at[1]),
+    )
+    early, late = slots * 3 // 8, slots - slots // 4
+    for copy in factor_loads:
+        copy.start()
+    for slot in range(early):
         load(slot).start()
     enter(("aux", "orb"))
+    for slot in range(early, slots):
+        load(slot).start()
+    for copy in factor_loads:
+        copy.wait()
     net = Net(sems["send"], sems["recv"])
 
     def part_rows(source, slot):
@@ -420,18 +432,18 @@
 
         return carry
 
-    early, late = slots // 4, slots - slots // 4
     lax.fori_loop(0, early, slot_step, 0)
 
-    half = slots // 2
+    half, pieces = slots // 2, 4
+    each = slots // pieces
     row = lax.broadcasted_iota(jnp.int32, table.shape[1:], 0)
-    for piece in range(2):
+    for piece in range(pieces):
         own_at = jnp.zeros(table.shape[1:], f32)
-        for slot in range(half):
-            value = (list_ref[0, piece * half + slot] - first_base).astype(f32)
+        for slot in range(each):
+            value = (list_ref[0, piece * each + slot] - first_base).astype(f32)
             own_at = jnp.where(row == slot, value, own_at)
-        table[2 * here + piece] = own_at
-    own_table = table.at[pl.ds(2 * here, 2)]
+        table[pieces * here + piece] = own_at
+    own_table = table.at[pl.ds(pieces * here, pieces)]
     table_copies = [
         net.copy(own_table, own_table, {"orb": (here + step) % size}) for step in range(1, size)
     ]
@@ -445,46 +457,35 @@
     gram_copies = net.spread("aux", orb_sum, rank // count)
     lax.fori_loop(late, slots, slot_step, 0)
 
-    if size > 2:
-
-        def pass_near(slot, carry):
-            forward(1, slot)
-            return carry
-
-        lax.fori_loop(0, slots, pass_near, 0)
     arrive(gram_copies)
     ridge = jnp.where(eye_mask(rank), ridge_weight, 0.0)
     work[...] = orb_sum[...] / (orb_rows * size) * room["s_nu"][...] + ridge
     panels = rank // PANEL
-    together = panels == slots
-
-    def beside(step):
-        if size > 3:
-            forward(2, step)
-
-    sweep_inverse(work, beside if together else None)
+    def beside_first(step):
+        if size > 2:
+            for at in range(-(-slots // panels)):
+                slot = step * -(-slots // panels) + at
+
+                @pl.when(slot < slots)
+                def _():
+                    forward(1, slot)
+
+    sweep_inverse(work, beside_first)
     for at, piece in enumerate(split_three(-work[...])):
         room["inverse"][at] = piece
-    for distance in range(3 if together else 2, size - 1):
-
-        def pass_on(slot, carry, distance=distance):
-            forward(distance, slot)
-            return carry
-
-        lax.fori_loop(0, slots, pass_on, 0)
     arrive(table_copies)
 
     def add_rows(source, piece, clear):
-        start = piece * half
-        rows = parts[pl.ds(aligned((source * slots + start) * edge, edge), half * edge), :]
+        start = piece * each
+        rows = parts[pl.ds(aligned((source * slots + start) * edge, edge), each * edge), :]
         inverse = tuple(room["inverse"][at] for at in range(3))
         room["q"][...] = dot_exact(split_three(rows), inverse)
-        places = table[2 * source + piece]
+        places = table[pieces * source + piece]
 
         def block_step(block, carry):
             name = jnp.full((1, rank), block, jnp.int32).astype(f32)
             total = jnp.zeros((edge, rank), f32) if clear else a_ref[block]
-            for slot in range(half):
+            for slot in range(each):
                 weight = jnp.where(places[slot:slot + 1, :] == name, 1.0, 0.0)
                 total += room["q"][slot * edge:(slot + 1) * edge, :] * weight
             a_ref[block] = total
@@ -492,25 +493,42 @@
 
         lax.fori_loop(0, a_ref.shape[0], block_step, 0)
 
-    add_rows(here, 0, True)
-    add_rows(here, 1, False)
+    for piece in range(pieces):
+        add_rows(here, piece, piece == 0)
+        if size > 3:
+            forward(2, piece)
 
     def source_step(at, carry):
+        if size > 3:
+
+            @pl.when(at == 1)
+            def _():
+                for slot in range(pieces, (pieces + slots) // 2):
+                    forward(2, slot)
+
+            @pl.when(at == 2)
+            def _():
+                for slot in range((pieces + slots) // 2, slots):
+                    forward(2, slot)
+                for far in range(3, size - 1):
+                    for slot in range(slots):
+                        forward(far, slot)
+
         distance, way = at // 2 + 1, 1 - at % 2 * 2
         source = here - way * distance
 
         @pl.when((source + size) // size * ((2 * size - 1 - source) // size) > 0)
         def _():
-            def half_step(piece, carry):
+            def piece_step(piece, carry):
                 @pl.when(place(way) == size - 1)
                 def _():
-                    for slot in range(half):
-                        landed(way, distance, piece * half + slot).wait_recv()
+                    for slot in range(each):
+                        landed(way, distance, piece * each + slot).wait_recv()
 
                 add_rows(source, piece, False)
                 return carry
 
-            lax.fori_loop(0, 2, half_step, 0)
+            lax.fori_loop(0, pieces, piece_step, 0)
 
         return carry
 
@@ -749,12 +767,14 @@
     square = (rank, rank)
     shapes = {
         "x": (slots, edge, tile_width),
+        "orb": (orb_rows // edge, edge, rank),
+        "nu": (nu_rows // edge, edge, rank),
         "parts": (orb_size * slots * edge, rank),
-        "table": (orb_size * 2, 8, rank),
+        "table": (orb_size * 4, 8, rank),
         "a": (first_rows // edge, edge, rank),
         "e": (slots, tile_width, rank),
         "part": (slots, edge, rank),
-        "q": (slots // 2 * edge, rank),
+        "q": (slots // 4 * edge, rank),
         "orb_land": (orb_size, rank // aux_size, rank),
         "gram_land": (aux_size, rank // aux_size, rank),
         "terms": (orb_rows, rank),
@@ -775,6 +795,7 @@
     dma = pltpu.SemaphoreType.DMA
     semaphores = {
         "x": dma((slots,)),
+        "factors": dma((2,)),
         "send": dma((net_count,)),
         "recv": dma((net_count,)),
         "hop_send": dma((2, orb_size - 1, slots)),
@@ -786,10 +807,10 @@
     vmem = pl.BlockSpec(memory_space=pltpu.VMEM)
     hbm = pl.BlockSpec(memory_space=pltpu.HBM)
 
-    def kernel(list_ref, x_hbm, orb_ref, nu_ref, a_out, b_out, c_out, scale_out, *scratch):
+    def kernel(list_ref, x_hbm, orb_hbm, nu_hbm, a_out, b_out, c_out, scale_out, *scratch):
         names = list(room)
         sweep_kernel(
-            edge, list_ref, x_hbm, orb_ref, nu_ref, a_out, b_out, c_out, scale_out,
+            edge, list_ref, x_hbm, orb_hbm, nu_hbm, a_out, b_out, c_out, scale_out,
             dict(zip(names, scratch)), dict(zip(semaphores, scratch[len(names):]))
         )
 
@@ -801,7 +822,7 @@
             jax.ShapeDtypeStruct((nu_rows, rank), f32),
             jax.ShapeDtypeStruct((8, rank), f32),
         ),
-        in_specs=[pl.BlockSpec(memory_space=pltpu.SMEM), hbm, vmem, vmem],
+        in_specs=[pl.BlockSpec(memory_space=pltpu.SMEM), hbm, hbm, hbm],
         out_specs=(hbm, hbm, vmem, vmem),
         scratch_shapes=list(room.values()) + list(semaphores.values()),
         compiler_params=pltpu.CompilerParams(

time: 109 us -> 111 us (1.018)
  Pallas kernels: 108 us -> 110 us
    pallas_call x1, Pallas kernels: 104 us -> 106 us  [per_device(): pl.pallas_call(kernel, out_shape=(jax.ShapeDtypeStruct((first_rows // edg...]
where the time goes in v7:
time: 111 us; the launch traced here: 110 us
  Pallas kernels  110 us (99%)
    pallas_call x1, Pallas kernels, per_device(): pl.pallas_call(kernel, out_shape=(jax.ShapeDtypeStruct((first_rows // edg...  106 us
    pallas_call x1, Pallas kernels, per_device(): pl.pallas_call(scale_kernel, out_shape=tuple((jax.ShapeDtypeStruct((size,...  3.73 us

profile of v7, /device:TPU:0, one launch (start us, length us, event | category | flops | bytes accessed | tf_op | source)
XLA Modules:
  0.0 110.5 jit_solution(2515699014918296159)
XLA Ops:
  0.6 106.0 %sweep.1 = (f32[32,64,256]{2,1,0:T(8,128)}, f32[1024,256]{1,0:T(8,128)}, f32[512,256]{1,0:T(8,128)}, f32[8,256]{1,0:T(8,128)}) custom-call(s32[4,8]{1,0:T(4,128)} %list_ref.1, f32[8,64,4096]{2,1,0:T(8,128)} %x_hbm.1, f32[16,64,256]{2,1,0:T(8,128)} %bitcast.4, f32[8,64,256]{2,1,0:T(8,128)} %bitcast.5), custom_call_target="tpu_custom_call" | custom-call | tf_op jit(solution)/shard_map/sweep/pallas_call | solution.py:817
  106.6 3.7 %scale.1 = (f32[2048,256]{1,0:T(8,128)}, f32[1024,256]{1,0:T(8,128)}, f32[512,256]{1,0:T(8,128)}) custom-call(f32[2048,256]{1,0:T(8,128)} %bitcast.3, f32[1024,256]{1,0:T(8,128)} %get-tuple-element.8.b_hbm, f32[512,256]{1,0:T(8,128)} %get-tuple-element.9.c_hbm, f32[8,256]{1,0:T(8,128)} %get-tuple-element.10.scale_ref), custom_call_target="tpu_custom_call" | custom-call | tf_op jit(solution)/shard_map/scale/pallas_call | solution.py:835

commit v8 on v7

--- a/solution.py
+++ b/solution.py
@@ -352,7 +352,7 @@
         pltpu.make_async_copy(nu_hbm, nu_ref, sems["factors"].at[0]),
         pltpu.make_async_copy(orb_hbm, orb_ref, sems["factors"].at[1]),
     )
-    early, late = slots * 3 // 8, slots - slots // 4
+    early, late = slots * 3 // 8, slots - 1
     for copy in factor_loads:
         copy.start()
     for slot in range(early):
@@ -688,7 +688,7 @@
 
     def beside_third(step):
         for when, act, side in (
-            (2, third_landed, 1), (panels - 3, third_summed, 0)
+            (2, third_landed, 1), (panels - 3, third_summed, 0), (panels - 1, third_summed, 1)
         ):
 
             @pl.when(step == when)
@@ -697,7 +697,6 @@
 
     sweep_inverse(work, beside_third)
     inverse = split_three(-work[...])
-    third_summed(1)
     for spread in spreads:
         spread.relay()
     for spread in spreads:

time: 111 us -> 110 us (level)
  no operation moved by 1% of the time
where the time goes in v8:
time: 110 us; the launch traced here: 109 us
  Pallas kernels  109 us (99%)
    pallas_call x1, Pallas kernels, per_device(): pl.pallas_call(kernel, out_shape=(jax.ShapeDtypeStruct((first_rows // edg...  105 us
    pallas_call x1, Pallas kernels, per_device(): pl.pallas_call(scale_kernel, out_shape=tuple((jax.ShapeDtypeStruct((size,...  3.73 us

profile of v8, /device:TPU:0, one launch (start us, length us, event | category | flops | bytes accessed | tf_op | source)
XLA Modules:
  0.0 109.5 jit_solution(5290095902640341980)
XLA Ops:
  0.6 104.9 %sweep.1 = (f32[32,64,256]{2,1,0:T(8,128)}, f32[1024,256]{1,0:T(8,128)}, f32[512,256]{1,0:T(8,128)}, f32[8,256]{1,0:T(8,128)}) custom-call(s32[4,8]{1,0:T(4,128)} %list_ref.1, f32[8,64,4096]{2,1,0:T(8,128)} %x_hbm.1, f32[16,64,256]{2,1,0:T(8,128)} %bitcast.4, f32[8,64,256]{2,1,0:T(8,128)} %bitcast.5), custom_call_target="tpu_custom_call" | custom-call | tf_op jit(solution)/shard_map/sweep/pallas_call | solution.py:816
  105.6 3.7 %scale.1 = (f32[2048,256]{1,0:T(8,128)}, f32[1024,256]{1,0:T(8,128)}, f32[512,256]{1,0:T(8,128)}) custom-call(f32[2048,256]{1,0:T(8,128)} %bitcast.3, f32[1024,256]{1,0:T(8,128)} %get-tuple-element.8.b_hbm, f32[512,256]{1,0:T(8,128)} %get-tuple-element.9.c_hbm, f32[8,256]{1,0:T(8,128)} %get-tuple-element.10.scale_ref), custom_call_target="tpu_custom_call" | custom-call | tf_op jit(solution)/shard_map/scale/pallas_call | solution.py:834

commit v9 on v8

--- a/solution.py
+++ b/solution.py
@@ -457,14 +457,21 @@
     gram_copies = net.spread("aux", orb_sum, rank // count)
     lax.fori_loop(late, slots, slot_step, 0)
 
+    if size > 2:
+
+        def pass_near(slot, carry):
+            forward(1, slot)
+            return carry
+
+        lax.fori_loop(0, half, pass_near, 0)
     arrive(gram_copies)
     ridge = jnp.where(eye_mask(rank), ridge_weight, 0.0)
     work[...] = orb_sum[...] / (orb_rows * size) * room["s_nu"][...] + ridge
     panels = rank // PANEL
     def beside_first(step):
         if size > 2:
-            for at in range(-(-slots // panels)):
-                slot = step * -(-slots // panels) + at
+            for at in range(-(-half // panels)):
+                slot = half + step * -(-half // panels) + at
 
                 @pl.when(slot < slots)
                 def _():
@@ -494,19 +501,19 @@
         lax.fori_loop(0, a_ref.shape[0], block_step, 0)
 
     for piece in range(pieces):
-        add_rows(here, piece, piece == 0)
         if size > 3:
             forward(2, piece)
+        add_rows(here, piece, piece == 0)
 
     def source_step(at, carry):
         if size > 3:
 
-            @pl.when(at == 1)
+            @pl.when(at == 0)
             def _():
                 for slot in range(pieces, (pieces + slots) // 2):
                     forward(2, slot)
 
-            @pl.when(at == 2)
+            @pl.when(at == 1)
             def _():
                 for slot in range((pieces + slots) // 2, slots):
                     forward(2, slot)

time: 110 us -> 107 us (0.973)
  Pallas kernels: 109 us -> 106 us
    pallas_call x1, Pallas kernels: 105 us -> 103 us  [per_device(): pl.pallas_call(kernel, out_shape=(jax.ShapeDtypeStruct((first_rows // edg...]
where the time goes in v9:
time: 107 us
  Pallas kernels  106 us (99%)
    pallas_call x1, Pallas kernels, per_device(): pl.pallas_call(kernel, out_shape=(jax.ShapeDtypeStruct((first_rows // edg...  103 us
    pallas_call x1, Pallas kernels, per_device(): pl.pallas_call(scale_kernel, out_shape=tuple((jax.ShapeDtypeStruct((size,...  3.73 us

profile of v9, /device:TPU:0, one launch (start us, length us, event | category | flops | bytes accessed | tf_op | source)
XLA Modules:
  0.0 107.3 jit_solution(6481553487502395047)
XLA Ops:
  0.6 102.8 %sweep.1 = (f32[32,64,256]{2,1,0:T(8,128)}, f32[1024,256]{1,0:T(8,128)}, f32[512,256]{1,0:T(8,128)}, f32[8,256]{1,0:T(8,128)}) custom-call(s32[4,8]{1,0:T(4,128)} %list_ref.1, f32[8,64,4096]{2,1,0:T(8,128)} %x_hbm.1, f32[16,64,256]{2,1,0:T(8,128)} %bitcast.4, f32[8,64,256]{2,1,0:T(8,128)} %bitcast.5), custom_call_target="tpu_custom_call" | custom-call | tf_op jit(solution)/shard_map/sweep/pallas_call | solution.py:823
  103.4 3.7 %scale.1 = (f32[2048,256]{1,0:T(8,128)}, f32[1024,256]{1,0:T(8,128)}, f32[512,256]{1,0:T(8,128)}) custom-call(f32[2048,256]{1,0:T(8,128)} %bitcast.3, f32[1024,256]{1,0:T(8,128)} %get-tuple-element.8.b_hbm, f32[512,256]{1,0:T(8,128)} %get-tuple-element.9.c_hbm, f32[8,256]{1,0:T(8,128)} %get-tuple-element.10.scale_ref), custom_call_target="tpu_custom_call" | custom-call | tf_op jit(solution)/shard_map/scale/pallas_call | solution.py:841
